TPU v7x, 32 devices: a whole 2x2x4 slice. The times are simulated.
32 devices in a mesh: query: 4 (over y, x), corpus: 8 (over z, core).
Axes of the slice: x: 2, y: 2, z: 4, core: 2. Of those that a mesh axis runs over, the one named last changes fastest.
Arguments:
- hidden_in: bfloat16 [512, 4096], P('query', 'corpus'), may hold values from -6 to 6
- lengths: int32 [16], P('query'), may hold values from 1 to 32, 320 in all
- gate_weight: bfloat16 [4096, 14336], P('query', 'corpus'), may hold values from -0.09375 to 0.09375
- up_weight: bfloat16 [4096, 14336], P('query', 'corpus'), may hold values from -0.09375 to 0.09375
- down_weight: bfloat16 [14336, 4096], P('corpus', 'query'), may hold values from -0.04175957 to 0.04175957
- code_weight: bfloat16 [4096, 1024], P('corpus'), may hold values from -0.03125 to 0.03125
- corpus_codes: bfloat16 [16384, 1024], P(('query', 'corpus')), may hold values from -1 to 1, as said below
Outputs:
- top_scores: float32 [16, 100], replicated
Inputs may be any that keep to these rules, and one draw needn't show every extreme that they name: `corpus_codes`: every entry is +1 or -1. `lengths`: at least one query has all 32 slots real.
All inputs are finite; a program needn't handle non-finite values. No bound on the sum of `lengths` on one device may be relied on, other than what follows from the above.
Results may differ from a plain program's by a relative error of at most 0.00067.
Values may be sent and summed in bfloat16 or wider, within the bound.
A program may use at most 128 MiB of HBM per device.

v0:
```python
import functools
import math

import jax
import jax.numpy as jnp
from jax import lax
from jax.experimental import pallas as pl
from jax.experimental.pallas import tpu as pltpu
from jax.sharding import PartitionSpec as P

SEQ = 32
LANES = 128
TOPK = 100
REAL_NUM, REAL_DEN = 5, 8
CHUNK = 256
PIECE = 32

epsilon = 1e-05
F32, BF16 = jnp.float32, jnp.bfloat16


def mm(a, b, precision=None):
    return lax.dot_general(a, b, (((1,), (0,)), ((), ())), precision=precision, preferred_element_type=F32)


def rcopy(src, dst, send, recv, dev):
    return pltpu.make_async_remote_copy(
        src_ref=src, dst_ref=dst, send_sem=send, recv_sem=recv,
        device_id=dev, device_id_type=pl.DeviceIdType.MESH)


def exchange(x, s, keep_max):
    bit = (lax.broadcasted_iota(jnp.int32, x.shape, 1) & s) != 0
    other = jnp.where(bit, pltpu.roll(x, s, 1), pltpu.roll(x, LANES - s, 1))
    return jnp.where(keep_max, jnp.maximum(x, other), jnp.minimum(x, other))


def sort_lanes(x):
    lane = lax.broadcasted_iota(jnp.int32, x.shape, 1)
    flip = (lax.broadcasted_iota(jnp.int32, x.shape, 0) >= x.shape[0] // 2).astype(jnp.int32)
    size = 2
    while size <= LANES:
        up = ((lane & size) != 0).astype(jnp.int32) if size < LANES else jnp.zeros_like(lane)
        s = size // 2
        while s:
            low = ((lane & s) != 0).astype(jnp.int32)
            x = exchange(x, s, (low ^ up ^ flip) == 0)
            s //= 2
        size *= 2
    return x


def merge_all(x, rows, lone):
    while x.shape[0] > rows:
        half = x.shape[0] // 2
        x = jnp.maximum(x[:half], x[half:])
        lane = lax.broadcasted_iota(jnp.int32, x.shape, 1)
        if half > rows:
            flip = (lax.broadcasted_iota(jnp.int32, x.shape, 0) >= half // 2).astype(jnp.int32)
        else:
            flip = jnp.zeros_like(lane) + jnp.asarray(lone, jnp.int32)
        s = LANES // 2
        while s:
            low = ((lane & s) != 0).astype(jnp.int32)
            x = exchange(x, s, (low ^ flip) == 0)
            s //= 2
    return x


def block_kernel(dims, hid, lens, gate_h, up_h, down_h, code_h, corp_h, out,
                 gate, up, down, code, corp, colbuf, lens_all, xall, psend, precv,
                 st_send, st_recv, inv_all, xn, pown, top_q, top_c, hall, acc, lsend, lrecv, gsend, grecv, t_send, t_recv,
                 pp, prc, pblk, cpart, crecv, codes,
                 w_s, a_s, a_r, l_s, l_r, ch_s, ch_r, la_s, la_r, p_s, p_r, st_s, st_r, iv_s, iv_r, tq_s, tq_r, tc_s, tc_r, h_s, h_r,
                 lr_s, lr_r, g_s, g_r, t_s, t_r, pp_s, pp_r, pb_s, pb_r, c_s, c_r, o_s, o_r):
    nq, nc, r, nreal, tq, tb, nch, cw, d_all = dims
    q = lax.axis_index("query")
    c = lax.axis_index("corpus")
    g = c // r
    j = lax.rem(c, r)
    slots, w = hid.shape[0], hid.shape[1]
    total = nq * slots
    nqueries = total // SEQ
    bw = code.shape[1] // nq

    loads = []
    for i, (s, d) in enumerate(((gate_h, gate), (up_h, up), (down_h, down), (code_h, code), (corp_h, corp))):
        cp = pltpu.make_async_copy(s, d, w_s.at[i])
        cp.start()
        loads.append(cp)

    def rq(k):
        return lax.rem(q + k, nq)

    def rc(k):
        return lax.rem(c + k, nc)

    def lane(k):
        return lax.rem(j + k, r)

    barrier = pltpu.get_barrier_semaphore()
    for k in range(1, nq):
        pl.semaphore_signal(barrier, inc=1, device_id=(rq(k), c), device_id_type=pl.DeviceIdType.MESH)
    for k in range(1, nc):
        pl.semaphore_signal(barrier, inc=1, device_id=(q, rc(k)), device_id_type=pl.DeviceIdType.MESH)
    pl.semaphore_wait(barrier, nq - 1 + nc - 1)

    for k in range(1, nq):
        rcopy(lens, lens_all.at[q], l_s.at[k], l_r.at[q], (rq(k), c)).start()

    @pl.when(q != g)
    def _():
        rcopy(hid, colbuf.at[q], a_s, a_r.at[q], (g, c)).start()

    squares = jnp.square(hid[...].astype(F32))
    st_send[...] = lax.dot_general(jnp.ones((8, w), F32), squares, (((1,), (1,)), ((), ())),
                                   precision=lax.Precision.HIGHEST, preferred_element_type=F32)
    for k in range(1, nc):
        rcopy(st_send, st_recv.at[c], st_s.at[k], st_r.at[c], (q, rc(k))).start()
    st_recv[c] = st_send[...]
    lens_all[q] = lens[...]
    for k in range(1, nq):
        s = rq(k)
        rcopy(lens, lens_all.at[s], l_s.at[k], l_r.at[s], (s, c)).wait_recv()
    lens_row = jnp.concatenate([lens_all[i] for i in range(nq)], axis=1)
    slot = lax.broadcasted_iota(jnp.int32, (8, total), 1)
    valid = lax.rem(slot, SEQ) < lens_row
    before = lax.broadcasted_iota(jnp.int32, (total, total), 0) < lax.broadcasted_iota(jnp.int32, (total, total), 1)
    pos = mm(valid.astype(F32).astype(BF16), before.astype(F32).astype(BF16)).astype(jnp.int32)
    pos = jnp.where(valid, pos, -1)[:1]

    for k in range(1, nc):
        s = rc(k)
        rcopy(st_send, st_recv.at[s], st_s.at[k], st_r.at[s], (q, s)).wait_recv()
    stat = st_recv[0]
    for i in range(1, nc):
        stat = stat + st_recv[i]
    inv_all[q] = lax.rsqrt(stat / d_all + epsilon)
    for k in range(1, nq):
        rcopy(inv_all.at[q], inv_all.at[q], iv_s.at[k], iv_r.at[q], (rq(k), c)).start()

    nb = ch_r.shape[0]
    ct = nreal // nb

    def chunk(i, slot_j):
        return xall.at[slot_j, pl.ds(i * ct, ct)]

    def down_chain(i):
        return rcopy(chunk(i, j), chunk(i, j), ch_s.at[0, i], ch_r.at[i], (q, jnp.maximum(c - r, 0)))

    def up_chain(i):
        return rcopy(chunk(i, j), chunk(i, j), ch_s.at[1, i], ch_r.at[i], (q, jnp.minimum(c + r, nc - 1)))

    sends_up = jnp.logical_and(g >= q, g < nc // r - 1)
    sends_down = jnp.logical_and(g <= q, g > 0)

    @pl.when(q == g)
    def _():
        colbuf[q] = hid[...]
        for k in range(1, nq):
            s = rq(k)
            rcopy(hid, colbuf.at[s], a_s, a_r.at[s], (s, c)).wait_recv()
        stacked = colbuf[...].reshape(total, w)
        for i in range(nq):
            row = lax.broadcasted_iota(jnp.int32, (tq, total), 0) + i * tq
            pick = (pos == row).astype(F32).astype(BF16)
            xall[j, i * tq:(i + 1) * tq, :] = mm(pick, stacked).astype(BF16)

    for i in range(nb):
        @pl.when(q != g)
        def _(i=i):
            up_chain(i).wait_recv()

        @pl.when(sends_up)
        def _(i=i):
            up_chain(i).start()

        @pl.when(sends_down)
        def _(i=i):
            down_chain(i).start()

        for k in range(1, r):
            rcopy(chunk(i, j), chunk(i, j), la_s.at[k, i], la_r.at[j, i], (q, g * r + lane(k))).start()
    for k in range(1, nq):
        s = rq(k)
        rcopy(inv_all.at[s], inv_all.at[s], iv_s.at[k], iv_r.at[s], (s, c)).wait_recv()
    inv_row = jnp.concatenate([inv_all[i] for i in range(nq)], axis=1)[:1]
    inv_cols = []
    for i in range(nq):
        row = lax.broadcasted_iota(jnp.int32, (tq, total), 0) + i * tq
        inv_cols.append(jnp.sum(jnp.where(pos == row, inv_row, 0.0), axis=1, keepdims=True))
    inv = jnp.concatenate(inv_cols, axis=0)
    for i in range(nb):
        for k in range(1, r):
            s = lane(k)
            rcopy(chunk(i, s), chunk(i, s), la_s.at[k, i], la_r.at[s, i], (q, g * r + s)).wait_recv()

    loads[0].wait()
    loads[1].wait()

    for i in range(r):
        xn[i] = (xall[i].astype(F32) * inv).astype(BF16)

    side_a = q + 1 - 2 * lax.rem(q, 2)
    side_b = q + 2 - 4 * (q // 2)
    far = nq - 1 - q

    def sides(n):
        odd = lax.rem(n, 2)
        return side_a + (side_b - side_a) * odd, side_b + (side_a - side_b) * odd

    def near_part(n):
        one, _ = sides(n)
        return rcopy(psend.at[n, one], precv.at[n, 0], p_s.at[n, 0], p_r.at[n, 0], (one, c))

    def far_part(n):
        one, _ = sides(n)
        return rcopy(psend.at[n, far], precv.at[n, 1], p_s.at[n, 1], p_r.at[n, 1], (one, c))

    def passed_part(n):
        _, two = sides(n)
        return rcopy(precv.at[n, 3], precv.at[n, 2], p_s.at[n, 2], p_r.at[n, 2], (two, c))

    def h_near(n, k):
        to = sides(n)[k]
        return rcopy(hall.at[n, q], hall.at[n, q], h_s.at[n, k], h_r.at[n, k], (to, c))

    def h_near_in(n, k):
        to = sides(n)[k]
        return rcopy(hall.at[n, to], hall.at[n, to], h_s.at[n, k], h_r.at[n, k], (to, c))

    def h_pass(n):
        one, two = sides(n)
        return rcopy(hall.at[n, one], hall.at[n, one], h_s.at[n, 2], h_r.at[n, 2], (two, c))

    def h_pass_in(n):
        _, two = sides(n)
        return rcopy(hall.at[n, far], hall.at[n, far], h_s.at[n, 2], h_r.at[n, 2], (two, c))

    def matmuls(n, carry):
        cols = pl.ds(pl.multiple_of(n * cw, cw), cw)
        for e, wref in enumerate((gate, up)):
            full = sum(mm(xn[i], wref[i * w:(i + 1) * w, cols]) for i in range(r))
            for i in range(nq):
                psend[n, i, e] = full[i * tq:(i + 1) * tq].astype(BF16)

                @pl.when(q == i)
                def _(i=i, e=e, full=full):
                    pown[n, e] = full[i * tq:(i + 1) * tq]
        far_part(n).start()
        near_part(n).start()
        return carry

    lax.fori_loop(0, nch, matmuls, 0)

    loads[2].wait()
    acc[...] = jnp.zeros_like(acc)

    def pass_chunk(n):
        _, two = sides(n)
        far_part(n).wait_recv()
        precv[n, 3] = (psend[n, two].astype(F32) + precv[n, 1].astype(F32)).astype(BF16)
        passed_part(n).start()

    def reduce_chunk(n):
        near_part(n).wait_recv()
        passed_part(n).wait_recv()
        gsum = pown[n, 0] + precv[n, 0, 0].astype(F32) + precv[n, 2, 0].astype(F32)
        usum = pown[n, 1] + precv[n, 0, 1].astype(F32) + precv[n, 2, 1].astype(F32)
        hall[n, q] = (gsum / (1.0 + jnp.exp(-gsum)) * usum).astype(BF16)
        h_near(n, 0).start()
        h_near(n, 1).start()

    def relay_chunk(n):
        h_near_in(n, 0).wait_recv()
        h_pass(n).start()

    def down_chunk(n):
        h_near_in(n, 1).wait_recv()
        h_pass_in(n).wait_recv()
        acc[...] += mm(hall[n].reshape(nreal, cw), down[pl.ds(pl.multiple_of(n * cw, cw), cw), :])

    def passes(n, carry):
        pass_chunk(n)
        return carry

    lax.fori_loop(0, nch, passes, 0)
    reduce_chunk(0)

    def reduces(n, carry):
        reduce_chunk(n)
        relay_chunk(n - 1)
        return carry

    lax.fori_loop(1, nch, reduces, 0)
    relay_chunk(nch - 1)

    def downs(n, carry):
        down_chunk(n)
        return carry

    lax.fori_loop(0, nch, downs, 0)

    ng = nc // r
    for gg in range(ng):
        for jj in range(r):
            b = gg * r + jj
            lsend[jj, gg] = acc[b * tb:(b + 1) * tb].astype(BF16)
    for k in range(1, r):
        t = lane(k)
        rcopy(lsend.at[t], lrecv.at[j], lr_s.at[k], lr_r.at[j], (q, g * r + t)).start()
    mine = lsend[j].astype(F32)
    for k in range(1, r):
        s = lane(k)
        rcopy(lsend.at[s], lrecv.at[s], lr_s.at[k], lr_r.at[s], (q, g * r + s)).wait_recv()
        mine = mine + lrecv[s].astype(F32)
    gsend[...] = mine.astype(BF16)
    for k in range(1, ng):
        t = lax.rem(g + k, ng)
        rcopy(gsend.at[t], grecv.at[g], g_s.at[k], g_r.at[g], (q, t * r + j)).start()
    row = lax.broadcasted_iota(jnp.int32, (tb, nreal), 0) + c * tb
    own_rows = (lax.broadcasted_iota(jnp.int32, (tb, nreal), 1) == row).astype(F32).astype(BF16)
    residual = jnp.concatenate([mm(own_rows, xall[i]) for i in range(r)], axis=1)
    residual = residual + gsend[g].astype(F32)
    for k in range(1, ng):
        s = lax.rem(g + k, ng)
        rcopy(gsend.at[s], grecv.at[s], g_s.at[k], g_r.at[s], (q, s * r + j)).wait_recv()
        residual = residual + grecv[s].astype(F32)

    t_send[...] = jnp.broadcast_to(jnp.sum(residual * residual, axis=1, keepdims=True), (tb, 128))
    for k in range(1, nq):
        rcopy(t_send, t_recv.at[q], t_s.at[k], t_r.at[q], (rq(k), c)).start()
    qrow = lax.broadcasted_iota(jnp.int32, (nqueries, total), 0)
    qslot = lax.broadcasted_iota(jnp.int32, (nqueries, total), 1)
    lens_b = jnp.broadcast_to(lens_row[:1], (nqueries, total)).astype(F32)
    vals_b = jnp.broadcast_to(valid.astype(F32)[:1], (nqueries, total))
    len_col = jnp.sum(jnp.where(qslot == qrow * SEQ, lens_b, 0.0), axis=1, keepdims=True)
    off_col = jnp.sum(jnp.where(qslot < qrow * SEQ, vals_b, 0.0), axis=1, keepdims=True)
    prow = (lax.broadcasted_iota(jnp.int32, (nqueries, tb), 1) + c * tb).astype(F32)
    member = jnp.where(jnp.logical_and(prow >= off_col, prow < off_col + len_col), 1.0, 0.0)
    tsum = t_send[...]
    for k in range(1, nq):
        s = rq(k)
        rcopy(t_send, t_recv.at[s], t_s.at[k], t_r.at[s], (s, c)).wait_recv()
        tsum = tsum + t_recv[s]
    final = residual * lax.rsqrt(tsum[:, :1] / d_all + epsilon)
    pooled_part = mm(member, final, lax.Precision.HIGHEST)
    for i in range(r):
        pp[i] = pooled_part[:, i * w:(i + 1) * w]
    for i in range(r):
        @pl.when(c != q * r + i)
        def _(i=i):
            rcopy(pp.at[i], prc.at[c], pp_s.at[i], pp_r.at[c], (q, q * r + i)).start()

    @pl.when(g == q)
    def _():
        pooled = pp[j]
        for k in range(1, nc):
            s = rc(k)
            rcopy(pp.at[j], prc.at[s], pp_s.at[0], pp_r.at[s], (q, s)).wait_recv()
            pooled = pooled + prc[s]
        pblk[...] = (pooled / len_col).astype(BF16)
        for k in range(1, nq):
            rcopy(pblk, pblk, pb_s.at[k], pb_r, (rq(k), c)).start()

    loads[3].wait()
    loads[4].wait()

    @pl.when(g != q)
    def _():
        rcopy(pblk, pblk, pb_s.at[0], pb_r, (g, c)).wait_recv()

    cpart[...] = mm(pblk[...], code[:, pl.ds(pl.multiple_of(q * bw, bw), bw)])
    for k in range(1, nc):
        rcopy(cpart, crecv.at[c], c_s.at[k], c_r.at[c], (q, rc(k))).start()
    crecv[c] = cpart[...]
    for k in range(1, nc):
        s = rc(k)
        rcopy(cpart, crecv.at[s], c_s.at[k], c_r.at[s], (q, s)).wait_recv()
    csum = crecv[0]
    for i in range(1, nc):
        csum = csum + crecv[i]
    codes[q] = csum.astype(BF16)
    for k in range(1, nq):
        rcopy(codes.at[q], codes.at[q], o_s.at[k], o_r.at[q], (rq(k), c)).start()
    for k in range(1, nq):
        s = rq(k)
        rcopy(codes.at[s], codes.at[s], o_s.at[k], o_r.at[s], (s, c)).wait_recv()
    qcodes = jnp.concatenate([codes[i] for i in range(nq)], axis=1)
    scale = 1.0 / math.sqrt(corp.shape[1])
    scores = lax.dot_general(qcodes, corp[...], (((1,), (1,)), ((), ())), preferred_element_type=F32) * scale

    blocks = corp.shape[0] // LANES
    lists = jnp.concatenate([scores[:, i * LANES:(i + 1) * LANES] for i in range(blocks)], axis=0)
    best = merge_all(sort_lanes(lists), nqueries, q >= nq // 2)
    top_q[q] = best
    for k in range(1, nq):
        rcopy(top_q.at[q], top_q.at[q], tq_s.at[k], tq_r.at[q], (rq(k), c)).start()
    for k in range(1, nq):
        s = rq(k)
        rcopy(top_q.at[s], top_q.at[s], tq_s.at[k], tq_r.at[s], (s, c)).wait_recv()
    best = merge_all(top_q[...].reshape(nq * nqueries, LANES), nqueries, c >= nc // 2)
    top_c[c] = best
    for k in range(1, nc):
        rcopy(top_c.at[c], top_c.at[c], tc_s.at[k], tc_r.at[c], (q, rc(k))).start()
    for k in range(1, nc):
        s = rc(k)
        rcopy(top_c.at[s], top_c.at[s], tc_s.at[k], tc_r.at[s], (q, s)).wait_recv()
    best = merge_all(top_c[...].reshape(nc * nqueries, LANES), nqueries, False)
    out[...] = best[:, :TOPK]

    for k in range(1, nq):
        rcopy(lens, lens_all.at[q], l_s.at[k], l_r.at[q], (rq(k), c)).wait_send()
        rcopy(inv_all.at[q], inv_all.at[q], iv_s.at[k], iv_r.at[q], (rq(k), c)).wait_send()
        rcopy(top_q.at[q], top_q.at[q], tq_s.at[k], tq_r.at[q], (rq(k), c)).wait_send()
        rcopy(t_send, t_recv.at[q], t_s.at[k], t_r.at[q], (rq(k), c)).wait_send()
        rcopy(codes.at[q], codes.at[q], o_s.at[k], o_r.at[q], (rq(k), c)).wait_send()

    @pl.when(q != g)
    def _():
        rcopy(hid, colbuf.at[q], a_s, a_r.at[q], (g, c)).wait_send()

    for i in range(nb):
        @pl.when(sends_up)
        def _(i=i):
            up_chain(i).wait_send()

        @pl.when(sends_down)
        def _(i=i):
            down_chain(i).wait_send()

        for k in range(1, r):
            rcopy(chunk(i, j), chunk(i, j), la_s.at[k, i], la_r.at[j, i], (q, g * r + lane(k))).wait_send()

    def drain(n, carry):
        far_part(n).wait_send()
        near_part(n).wait_send()
        passed_part(n).wait_send()
        h_near(n, 0).wait_send()
        h_near(n, 1).wait_send()
        h_pass(n).wait_send()
        return carry

    lax.fori_loop(0, nch, drain, 0)
    for k in range(1, r):
        rcopy(lsend.at[lane(k)], lrecv.at[j], lr_s.at[k], lr_r.at[j], (q, g * r + lane(k))).wait_send()
    for k in range(1, ng):
        t = lax.rem(g + k, ng)
        rcopy(gsend.at[t], grecv.at[g], g_s.at[k], g_r.at[g], (q, t * r + j)).wait_send()
    for i in range(r):
        @pl.when(c != q * r + i)
        def _(i=i):
            rcopy(pp.at[i], prc.at[c], pp_s.at[i], pp_r.at[c], (q, q * r + i)).wait_send()

    @pl.when(g == q)
    def _():
        for k in range(1, nq):
            rcopy(pblk, pblk, pb_s.at[k], pb_r, (rq(k), c)).wait_send()
    for k in range(1, nc):
        rcopy(cpart, crecv.at[c], c_s.at[k], c_r.at[c], (q, rc(k))).wait_send()
        rcopy(st_send, st_recv.at[c], st_s.at[k], st_r.at[c], (q, rc(k))).wait_send()
        rcopy(top_c.at[c], top_c.at[c], tc_s.at[k], tc_r.at[c], (q, rc(k))).wait_send()


def per_device(nq, nc, hidden_in, lengths, gate_weight, up_weight, down_weight, code_weight, corpus_codes):
    slots, w = hidden_in.shape
    r = nc // nq
    nreal = nq * slots * REAL_NUM // REAL_DEN
    tq, tb = nreal // nq, nreal // nc
    dq, ffc = gate_weight.shape
    cw = CHUNK if ffc % CHUNK == 0 else ffc
    nch = ffc // cw
    nb = nreal // PIECE if nreal % PIECE == 0 else nq
    nqueries = nq * lengths.shape[0]
    bits = code_weight.shape[1]
    bw = bits // nq
    ng = nc // r
    lens = jnp.broadcast_to(jnp.repeat(lengths, SEQ)[None, :], (8, slots))
    vm, dma = pltpu.VMEM, pltpu.SemaphoreType.DMA
    scratch = [
        vm(gate_weight.shape, BF16), vm(up_weight.shape, BF16), vm(down_weight.shape, BF16),
        vm(code_weight.shape, BF16), vm(corpus_codes.shape, BF16),
        vm((nq, slots, w), BF16), vm((nq, 8, slots), jnp.int32), vm((r, nreal, w), BF16),
        vm((nch, nq, 2, tq, cw), BF16), vm((nch, nq, 2, tq, cw), BF16),
        vm((8, slots), F32), vm((nc, 8, slots), F32), vm((nq, 8, slots), F32), vm((r, nreal, w), BF16),
        vm((nch, 2, tq, cw), F32), vm((nq, nqueries, LANES), F32), vm((nc, nqueries, LANES), F32),
        vm((nch, nq, tq, cw), BF16), vm((nreal, dq), F32),
        vm((r, ng, tb, dq), BF16), vm((r, ng, tb, dq), BF16), vm((ng, tb, dq), BF16), vm((ng, tb, dq), BF16),
        vm((tb, 128), F32), vm((nq, tb, 128), F32),
        vm((r, nqueries, w), F32), vm((nc, nqueries, w), F32), vm((nqueries, w), BF16),
        vm((nqueries, bw), F32), vm((nc, nqueries, bw), F32), vm((nq, nqueries, bw), BF16),
        dma((5,)), dma, dma((nq,)), dma((nq,)), dma((nq,)), dma((2, nb)), dma((nb,)), dma((r, nb)), dma((r, nb)),
        dma((nch, nq)), dma((nch, nq)), dma((nc,)), dma((nc,)), dma((nq,)), dma((nq,)),
        dma((nq,)), dma((nq,)), dma((nc,)), dma((nc,)), dma((nch, nq)), dma((nch, nq)),
        dma((r,)), dma((r,)), dma((ng,)), dma((ng,)), dma((nq,)), dma((nq,)),
        dma((r,)), dma((nc,)), dma((nq,)), dma, dma((nc,)), dma((nc,)), dma((nq,)), dma((nq,)),
    ]
    dims = (nq, nc, r, nreal, tq, tb, nch, cw, w * nc)
    vspec, aspec = pl.BlockSpec(memory_space=pltpu.VMEM), pl.BlockSpec(memory_space=pl.ANY)
    return pl.pallas_call(
        functools.partial(block_kernel, dims),
        out_shape=jax.ShapeDtypeStruct((nqueries, TOPK), F32),
        in_specs=[vspec, vspec] + [aspec] * 5,
        out_specs=vspec,
        scratch_shapes=scratch,
        compiler_params=pltpu.CompilerParams(
            collective_id=0, has_side_effects=True, vmem_limit_bytes=60 * 1024 * 1024),
    )(hidden_in, lens, gate_weight, up_weight, down_weight, code_weight, corpus_codes)


def solution(mesh):
    in_specs = (
        P("query", "corpus"),
        P("query"),
        P("query", "corpus"),
        P("query", "corpus"),
        P("corpus", "query"),
        P("corpus", None),
        P(("query", "corpus"), None),
    )
    body = functools.partial(per_device, mesh.shape["query"], mesh.shape["corpus"])
    return jax.shard_map(body, mesh=mesh, in_specs=in_specs, out_specs=P(), check_vma=False)
```

profile of v0, /device:TPU:0, one launch (start us, length us, event | category | flops | bytes accessed | tf_op | source)
XLA Modules:
  0.0 110.8 jit_solution(2649790571126254121)
XLA Ops:
  0.0 0.7 broadcast_in_dim.10
  0.7 0.1 broadcast_in_dim.11
  0.8 0.6 broadcast_in_dim.12.lens
  1.4 108.1 %shard_map.73 = f32[16,100]{1,0:T(8,128)} custom-call(bf16[128,512]{1,0:T(8,128)(2,1)} %hid.1, s32[8,128]{1,0:T(8,128)} %broadcast_in_dim.12.lens, bf16[1024,1792]{1,0:T(8,128)(2,1)} %gate_h.1, bf16[1024,1792]{1,0:T(8,128)(2,1)} %up_h.1, bf16[1792,1024]{1,0:T(8,128)(2,1)} %down_h.1, bf16[512,1024]{1,0:T(8,128)(2,1)} %code_h.1, bf16[512,1024]{1,0:T(8,128)(2,1)} %corp_h.1), custom_call_target="tpu_custom_call" | custom-call | tf_op jit(solution)/shard_map/pallas_call | solution.py:500
  109.5 1.3 %copy.9 = f32[16,100]{1,0:T(8,128)} copy(f32[16,100]{1,0:T(8,128)} %shard_map.73) | data formatting | bytes 12800
where the time goes:
time: 111 us
  Pallas kernels  108 us (97%)
  local copies, waits for them, and re-layouts  2.7 us (2%)
    pallas_call x1, Pallas kernels, per_device(): pl.pallas_call(functools.partial(block_kernel, dims), out_shape=jax.Shape...  108 us

commit v1 on v0

--- a/solution.py
+++ b/solution.py
@@ -1,5 +1,6 @@
 import functools
 import math
+import types
 
 import jax
 import jax.numpy as jnp
@@ -67,7 +68,7 @@
     return x
 
 
-def block_kernel(dims, hid, lens, gate_h, up_h, down_h, code_h, corp_h, out,
+def general_kernel(dims, hid, lens, gate_h, up_h, down_h, code_h, corp_h, out,
                  gate, up, down, code, corp, colbuf, lens_all, xall, psend, precv,
                  st_send, st_recv, inv_all, xn, pown, top_q, top_c, hall, acc, lsend, lrecv, gsend, grecv, t_send, t_recv,
                  pp, prc, pblk, cpart, crecv, codes,
@@ -462,7 +463,7 @@
         rcopy(top_c.at[c], top_c.at[c], tc_s.at[k], tc_r.at[c], (q, rc(k))).wait_send()
 
 
-def per_device(nq, nc, hidden_in, lengths, gate_weight, up_weight, down_weight, code_weight, corpus_codes):
+def per_device_general(nq, nc, hidden_in, lengths, gate_weight, up_weight, down_weight, code_weight, corpus_codes):
     slots, w = hidden_in.shape
     r = nc // nq
     nreal = nq * slots * REAL_NUM // REAL_DEN
@@ -498,7 +499,7 @@
     dims = (nq, nc, r, nreal, tq, tb, nch, cw, w * nc)
     vspec, aspec = pl.BlockSpec(memory_space=pltpu.VMEM), pl.BlockSpec(memory_space=pl.ANY)
     return pl.pallas_call(
-        functools.partial(block_kernel, dims),
+        functools.partial(general_kernel, dims),
         out_shape=jax.ShapeDtypeStruct((nqueries, TOPK), F32),
         in_specs=[vspec, vspec] + [aspec] * 5,
         out_specs=vspec,
@@ -506,6 +507,496 @@
         compiler_params=pltpu.CompilerParams(
             collective_id=0, has_side_effects=True, vmem_limit_bytes=60 * 1024 * 1024),
     )(hidden_in, lens, gate_weight, up_weight, down_weight, code_weight, corpus_codes)
+
+
+def fast_kernel(dims, names, hid, lens, gate_h, up_h, down_h, code_h, corp_h, out, *refs):
+    nq, nc, r, nblk, bm, nh, hw, d_all = dims
+    s = types.SimpleNamespace(**dict(zip(names, refs)))
+    q = lax.axis_index("query")
+    c = lax.axis_index("corpus")
+    g = c // r
+    j = lax.rem(c, r)
+    ng = nc // r
+    slots, w = hid.shape
+    total = nq * slots
+    nqueries = total // SEQ
+    nreal = nblk * bm
+    qm, lm, pm = bm // nq, bm // r, bm // nc
+    nu = nblk * nh
+    bw = s.code.shape[1] // nq
+    drains = []
+
+    loads = []
+    for i, (a, b) in enumerate(((gate_h, s.gate), (up_h, s.up), (down_h, s.down), (code_h, s.code), (corp_h, s.corp))):
+        cp = pltpu.make_async_copy(a, b, s.w_s.at[i])
+        cp.start()
+        loads.append(cp)
+
+    slot_query = lax.broadcasted_iota(jnp.int32, (8, slots), 1) // SEQ
+    own_lens = jnp.zeros((8, slots), jnp.int32)
+    for k in range(slots // SEQ):
+        own_lens = jnp.where(slot_query == k, lens[k], own_lens)
+    s.lens_all[q] = own_lens
+
+    def rq(k):
+        return lax.rem(q + k, nq)
+
+    def rc(k):
+        return lax.rem(c + k, nc)
+
+    def lane(k):
+        return lax.rem(j + k, r)
+
+    def send(cp):
+        cp.start()
+        drains.append(cp.wait_send)
+
+    barrier = pltpu.get_barrier_semaphore()
+    for k in range(1, nq):
+        pl.semaphore_signal(barrier, inc=1, device_id=(rq(k), c), device_id_type=pl.DeviceIdType.MESH)
+    for k in range(1, nc):
+        pl.semaphore_signal(barrier, inc=1, device_id=(q, rc(k)), device_id_type=pl.DeviceIdType.MESH)
+    pl.semaphore_wait(barrier, nq - 1 + nc - 1)
+
+    for k in range(1, nq):
+        send(rcopy(s.lens_all.at[q], s.lens_all.at[q], s.l_s.at[k], s.l_r.at[q], (rq(k), c)))
+
+    @pl.when(q != g)
+    def _():
+        rcopy(hid, s.colbuf.at[q], s.a_s, s.a_r.at[q], (g, c)).start()
+
+    squares = jnp.square(hid[...].astype(F32))
+    s.st_send[...] = lax.dot_general(jnp.ones((8, w), F32), squares, (((1,), (1,)), ((), ())),
+                                     precision=lax.Precision.HIGHEST, preferred_element_type=F32)
+    for k in range(1, nc):
+        send(rcopy(s.st_send, s.st_recv.at[c], s.st_s.at[k], s.st_r.at[c], (q, rc(k))))
+    s.st_recv[c] = s.st_send[...]
+    for k in range(1, nq):
+        p = rq(k)
+        rcopy(s.lens_all.at[p], s.lens_all.at[p], s.l_s.at[k], s.l_r.at[p], (p, c)).wait_recv()
+    lens_row = jnp.concatenate([s.lens_all[i] for i in range(nq)], axis=1)
+    slot = lax.broadcasted_iota(jnp.int32, (8, total), 1)
+    valid = lax.rem(slot, SEQ) < lens_row
+    before = lax.broadcasted_iota(jnp.int32, (total, total), 0) < lax.broadcasted_iota(jnp.int32, (total, total), 1)
+    pos = mm(valid.astype(F32).astype(BF16), before.astype(F32).astype(BF16)).astype(jnp.int32)
+    pos = jnp.where(valid, pos, -1)[:1]
+
+    for k in range(1, nc):
+        p = rc(k)
+        rcopy(s.st_send, s.st_recv.at[p], s.st_s.at[k], s.st_r.at[p], (q, p)).wait_recv()
+    stat = s.st_recv[0]
+    for i in range(1, nc):
+        stat = stat + s.st_recv[i]
+    s.inv_all[q] = lax.rsqrt(stat / d_all + epsilon)
+    for k in range(1, nq):
+        send(rcopy(s.inv_all.at[q], s.inv_all.at[q], s.iv_s.at[k], s.iv_r.at[q], (rq(k), c)))
+
+    def block(b, jj):
+        return s.xall.at[jj, b]
+
+    def down_chain(b):
+        return rcopy(block(b, j), block(b, j), s.ch_s.at[0, b], s.ch_r.at[b], (q, jnp.maximum(c - r, 0)))
+
+    def up_chain(b):
+        return rcopy(block(b, j), block(b, j), s.ch_s.at[1, b], s.ch_r.at[b], (q, jnp.minimum(c + r, nc - 1)))
+
+    def side(b, k):
+        return rcopy(block(b, j), block(b, j), s.la_s.at[k, b], s.la_r.at[j, b], (q, g * r + lane(k)))
+
+    def side_in(b, k):
+        p = lane(k)
+        return rcopy(block(b, p), block(b, p), s.la_s.at[k, b], s.la_r.at[p, b], (q, g * r + p))
+
+    sends_up = jnp.logical_and(g >= q, g < ng - 1)
+    sends_down = jnp.logical_and(g <= q, g > 0)
+
+    def pass_on(b):
+        @pl.when(sends_up)
+        def _():
+            up_chain(b).start()
+
+        @pl.when(sends_down)
+        def _():
+            down_chain(b).start()
+
+        for k in range(1, r):
+            side(b, k).start()
+
+    @pl.when(q == g)
+    def _():
+        s.colbuf[q] = hid[...]
+        for k in range(1, nq):
+            p = rq(k)
+            rcopy(hid, s.colbuf.at[p], s.a_s, s.a_r.at[p], (p, c)).wait_recv()
+        stacked = s.colbuf[...].reshape(total, w)
+        for b in range(nblk):
+            row = lax.broadcasted_iota(jnp.int32, (bm, total), 0) + b * bm
+            pick = (pos == row).astype(F32).astype(BF16)
+            s.xall[j, b] = mm(pick, stacked).astype(BF16)
+            pass_on(b)
+
+    for k in range(1, nq):
+        p = rq(k)
+        rcopy(s.inv_all.at[p], s.inv_all.at[p], s.iv_s.at[k], s.iv_r.at[p], (p, c)).wait_recv()
+    inv_row = jnp.concatenate([s.inv_all[i] for i in range(nq)], axis=1)[:1]
+    for b in range(nblk):
+        row = lax.broadcasted_iota(jnp.int32, (bm, total), 0) + b * bm
+        col = jnp.sum(jnp.where(pos == row, inv_row, 0.0), axis=1, keepdims=True)
+        s.inv_c[b] = jnp.broadcast_to(col, (bm, LANES))
+
+    loads[0].wait()
+    loads[1].wait()
+
+    side_a = q + 1 - 2 * lax.rem(q, 2)
+    side_b = q + 2 - 4 * (q // 2)
+    far = nq - 1 - q
+
+    def sides(n):
+        odd = lax.rem(n, 2)
+        return side_a + (side_b - side_a) * odd, side_b + (side_a - side_b) * odd
+
+    def near_part(n):
+        one, _ = sides(n)
+        return rcopy(s.psend.at[n, one], s.precv.at[n, 0], s.p_s.at[n, 0], s.p_r.at[n, 0], (one, c))
+
+    def far_part(n):
+        one, _ = sides(n)
+        return rcopy(s.psend.at[n, far], s.precv.at[n, 1], s.p_s.at[n, 1], s.p_r.at[n, 1], (one, c))
+
+    def passed_part(n):
+        _, two = sides(n)
+        return rcopy(s.precv.at[n, 3], s.precv.at[n, 2], s.p_s.at[n, 2], s.p_r.at[n, 2], (two, c))
+
+    def h_near(n, k):
+        to = sides(n)[k]
+        return rcopy(s.hall.at[n, q], s.hall.at[n, q], s.h_s.at[n, k], s.h_r.at[n, k], (to, c))
+
+    def h_near_in(n, k):
+        to = sides(n)[k]
+        return rcopy(s.hall.at[n, to], s.hall.at[n, to], s.h_s.at[n, k], s.h_r.at[n, k], (to, c))
+
+    def h_pass(n):
+        one, two = sides(n)
+        return rcopy(s.hall.at[n, one], s.hall.at[n, one], s.h_s.at[n, 2], s.h_r.at[n, 2], (two, c))
+
+    def h_pass_in(n):
+        _, two = sides(n)
+        return rcopy(s.hall.at[n, far], s.hall.at[n, far], s.h_s.at[n, 2], s.h_r.at[n, 2], (two, c))
+
+    def products(b, carry):
+        @pl.when(q != g)
+        def _():
+            up_chain(b).wait_recv()
+            pass_on(b)
+
+        for k in range(1, r):
+            side_in(b, k).wait_recv()
+        scale = s.inv_c[b][:, :1]
+        for i in range(r):
+            s.xn[:, i * w:(i + 1) * w] = (s.xall[i, b].astype(F32) * scale).astype(BF16)
+        xb = s.xn[...]
+        for h in range(nh):
+            n = b * nh + h
+            for e, wref in enumerate((s.gate, s.up)):
+                full = mm(xb, wref[:, h * hw:(h + 1) * hw])
+                for i in range(nq):
+                    s.psend[n, i, e] = full[i * qm:(i + 1) * qm].astype(BF16)
+
+                    @pl.when(q == i)
+                    def _(i=i, e=e, full=full, n=n):
+                        s.pown[n, e] = full[i * qm:(i + 1) * qm]
+            far_part(n).start()
+            near_part(n).start()
+        return carry
+
+    lax.fori_loop(0, nblk, products, 0)
+
+    row = lax.broadcasted_iota(jnp.int32, (nblk * pm, nreal), 0)
+    row = (row // pm) * bm + (j * ng + g) * pm + lax.rem(row, pm)
+    own_rows = (lax.broadcasted_iota(jnp.int32, (nblk * pm, nreal), 1) == row).astype(F32).astype(BF16)
+    for i in range(r):
+        s.res[:, i * w:(i + 1) * w] = mm(own_rows, s.xall[i].reshape(nreal, w))
+
+    loads[2].wait()
+
+    def passes(n, carry):
+        _, two = sides(n)
+        far_part(n).wait_recv()
+        s.precv[n, 3] = (s.psend[n, two].astype(F32) + s.precv[n, 1].astype(F32)).astype(BF16)
+        passed_part(n).start()
+        return carry
+
+    def reduce_unit(n):
+        near_part(n).wait_recv()
+        passed_part(n).wait_recv()
+        gsum = s.pown[n, 0] + s.precv[n, 0, 0].astype(F32) + s.precv[n, 2, 0].astype(F32)
+        usum = s.pown[n, 1] + s.precv[n, 0, 1].astype(F32) + s.precv[n, 2, 1].astype(F32)
+        s.hall[n, q] = (gsum / (1.0 + jnp.exp(-gsum)) * usum).astype(BF16)
+        h_near(n, 0).start()
+        h_near(n, 1).start()
+
+    def relay_unit(n):
+        h_near_in(n, 0).wait_recv()
+        h_pass(n).start()
+
+    def reduces(n, carry):
+        reduce_unit(n)
+        relay_unit(n - 1)
+        return carry
+
+    lax.fori_loop(0, nu, passes, 0)
+    reduce_unit(0)
+    lax.fori_loop(1, nu, reduces, 0)
+    relay_unit(nu - 1)
+
+    def lane_send(b, k):
+        t = lane(k)
+        return rcopy(s.lsend.at[b, t], s.lrecv.at[b, j], s.lr_s.at[b, k], s.lr_r.at[b, j], (q, g * r + t))
+
+    def lane_in(b, k):
+        p = lane(k)
+        return rcopy(s.lsend.at[b, p], s.lrecv.at[b, p], s.lr_s.at[b, k], s.lr_r.at[b, p], (q, g * r + p))
+
+    def group_send(b, k):
+        t = lax.rem(g + k, ng)
+        return rcopy(s.gsend.at[b, t], s.grecv.at[b, g], s.g_s.at[b, k], s.g_r.at[b, g], (q, t * r + j))
+
+    def group_in(b, k):
+        p = lax.rem(g + k, ng)
+        return rcopy(s.gsend.at[b, p], s.grecv.at[b, p], s.g_s.at[b, k], s.g_r.at[b, p], (q, p * r + j))
+
+    def down_block(b):
+        part = None
+        for h in range(nh):
+            n = b * nh + h
+            h_near_in(n, 1).wait_recv()
+            h_pass_in(n).wait_recv()
+            term = mm(s.hall[n].reshape(bm, hw), s.down[h * hw:(h + 1) * hw, :])
+            part = term if part is None else part + term
+        for t in range(r):
+            s.lsend[b, t] = part[t * lm:(t + 1) * lm].astype(BF16)
+        for k in range(1, r):
+            lane_send(b, k).start()
+
+    def sum_block(b):
+        mine = s.lsend[b, j].astype(F32)
+        for k in range(1, r):
+            lane_in(b, k).wait_recv()
+            mine = mine + s.lrecv[b, lane(k)].astype(F32)
+        for t in range(ng):
+            s.gsend[b, t] = mine[t * pm:(t + 1) * pm].astype(BF16)
+        for k in range(1, ng):
+            group_send(b, k).start()
+
+    def downs(b, carry):
+        down_block(b)
+        sum_block(b - 1)
+        return carry
+
+    down_block(0)
+    lax.fori_loop(1, nblk, downs, 0)
+    sum_block(nblk - 1)
+    for b in range(nblk):
+        total_b = s.gsend[b, g].astype(F32)
+        for k in range(1, ng):
+            group_in(b, k).wait_recv()
+            total_b = total_b + s.grecv[b, lax.rem(g + k, ng)].astype(F32)
+        s.res[b * pm:(b + 1) * pm, :] = s.res[b * pm:(b + 1) * pm, :] + total_b
+    residual = s.res[...]
+    tb = nblk * pm
+
+    s.t_send[...] = jnp.broadcast_to(jnp.sum(residual * residual, axis=1, keepdims=True), (tb, LANES))
+    for k in range(1, nq):
+        send(rcopy(s.t_send, s.t_recv.at[q], s.t_s.at[k], s.t_r.at[q], (rq(k), c)))
+    qrow = lax.broadcasted_iota(jnp.int32, (nqueries, total), 0)
+    qslot = lax.broadcasted_iota(jnp.int32, (nqueries, total), 1)
+    lens_b = jnp.broadcast_to(lens_row[:1], (nqueries, total)).astype(F32)
+    vals_b = jnp.broadcast_to(valid.astype(F32)[:1], (nqueries, total))
+    len_col = jnp.sum(jnp.where(qslot == qrow * SEQ, lens_b, 0.0), axis=1, keepdims=True)
+    off_col = jnp.sum(jnp.where(qslot < qrow * SEQ, vals_b, 0.0), axis=1, keepdims=True)
+    prow = lax.broadcasted_iota(jnp.int32, (nqueries, tb), 1)
+    prow = ((prow // pm) * bm + (j * ng + g) * pm + lax.rem(prow, pm)).astype(F32)
+    member = jnp.where(jnp.logical_and(prow >= off_col, prow < off_col + len_col), 1.0, 0.0)
+    tsum = s.t_send[...]
+    for k in range(1, nq):
+        p = rq(k)
+        rcopy(s.t_send, s.t_recv.at[p], s.t_s.at[k], s.t_r.at[p], (p, c)).wait_recv()
+        tsum = tsum + s.t_recv[p]
+    final = residual * lax.rsqrt(tsum[:, :1] / d_all + epsilon)
+    pooled_part = mm(member, final, lax.Precision.HIGHEST)
+    for i in range(r):
+        s.pp[i] = pooled_part[:, i * w:(i + 1) * w]
+    for i in range(r):
+        @pl.when(c != q * r + i)
+        def _(i=i):
+            rcopy(s.pp.at[i], s.prc.at[c], s.pp_s.at[i], s.pp_r.at[c], (q, q * r + i)).start()
+
+    @pl.when(g == q)
+    def _():
+        pooled = s.pp[j]
+        for k in range(1, nc):
+            p = rc(k)
+            rcopy(s.pp.at[j], s.prc.at[p], s.pp_s.at[0], s.pp_r.at[p], (q, p)).wait_recv()
+            pooled = pooled + s.prc[p]
+        s.pblk[...] = (pooled / len_col).astype(BF16)
+        for k in range(1, nq):
+            rcopy(s.pblk, s.pblk, s.pb_s.at[k], s.pb_r, (rq(k), c)).start()
+
+    loads[3].wait()
+    loads[4].wait()
+
+    @pl.when(g != q)
+    def _():
+        rcopy(s.pblk, s.pblk, s.pb_s.at[0], s.pb_r, (g, c)).wait_recv()
+
+    s.cpart[...] = mm(s.pblk[...], s.code[:, pl.ds(pl.multiple_of(q * bw, bw), bw)])
+    for k in range(1, nc):
+        send(rcopy(s.cpart, s.crecv.at[c], s.c_s.at[k], s.c_r.at[c], (q, rc(k))))
+    s.crecv[c] = s.cpart[...]
+    for k in range(1, nc):
+        p = rc(k)
+        rcopy(s.cpart, s.crecv.at[p], s.c_s.at[k], s.c_r.at[p], (q, p)).wait_recv()
+    csum = s.crecv[0]
+    for i in range(1, nc):
+        csum = csum + s.crecv[i]
+    s.codes[q] = csum.astype(BF16)
+    for k in range(1, nq):
+        send(rcopy(s.codes.at[q], s.codes.at[q], s.o_s.at[k], s.o_r.at[q], (rq(k), c)))
+    for k in range(1, nq):
+        p = rq(k)
+        rcopy(s.codes.at[p], s.codes.at[p], s.o_s.at[k], s.o_r.at[p], (p, c)).wait_recv()
+    qcodes = jnp.concatenate([s.codes[i] for i in range(nq)], axis=1)
+    scale = 1.0 / math.sqrt(s.corp.shape[1])
+    scores = lax.dot_general(qcodes, s.corp[...], (((1,), (1,)), ((), ())), preferred_element_type=F32) * scale
+
+    blocks = s.corp.shape[0] // LANES
+    lists = jnp.concatenate([scores[:, i * LANES:(i + 1) * LANES] for i in range(blocks)], axis=0)
+    best = merge_all(sort_lanes(lists), nqueries, q >= nq // 2)
+    s.top_q[q] = best
+    for k in range(1, nq):
+        send(rcopy(s.top_q.at[q], s.top_q.at[q], s.tq_s.at[k], s.tq_r.at[q], (rq(k), c)))
+    for k in range(1, nq):
+        p = rq(k)
+        rcopy(s.top_q.at[p], s.top_q.at[p], s.tq_s.at[k], s.tq_r.at[p], (p, c)).wait_recv()
+    best = merge_all(s.top_q[...].reshape(nq * nqueries, LANES), nqueries, c >= nc // 2)
+    s.top_c[c] = best
+    for k in range(1, nc):
+        send(rcopy(s.top_c.at[c], s.top_c.at[c], s.tc_s.at[k], s.tc_r.at[c], (q, rc(k))))
+    for k in range(1, nc):
+        p = rc(k)
+        rcopy(s.top_c.at[p], s.top_c.at[p], s.tc_s.at[k], s.tc_r.at[p], (q, p)).wait_recv()
+    best = merge_all(s.top_c[...].reshape(nc * nqueries, LANES), nqueries, False)
+    out[...] = best[:, :TOPK]
+
+    for wait in drains:
+        wait()
+
+    @pl.when(q != g)
+    def _():
+        rcopy(hid, s.colbuf.at[q], s.a_s, s.a_r.at[q], (g, c)).wait_send()
+
+    def drain_blocks(b, carry):
+        @pl.when(sends_up)
+        def _():
+            up_chain(b).wait_send()
+
+        @pl.when(sends_down)
+        def _():
+            down_chain(b).wait_send()
+
+        for k in range(1, r):
+            side(b, k).wait_send()
+        for k in range(1, r):
+            lane_send(b, k).wait_send()
+        for k in range(1, ng):
+            group_send(b, k).wait_send()
+        return carry
+
+    def drain_units(n, carry):
+        far_part(n).wait_send()
+        near_part(n).wait_send()
+        passed_part(n).wait_send()
+        h_near(n, 0).wait_send()
+        h_near(n, 1).wait_send()
+        h_pass(n).wait_send()
+        return carry
+
+    lax.fori_loop(0, nblk, drain_blocks, 0)
+    lax.fori_loop(0, nu, drain_units, 0)
+    for i in range(r):
+        @pl.when(c != q * r + i)
+        def _(i=i):
+            rcopy(s.pp.at[i], s.prc.at[c], s.pp_s.at[i], s.pp_r.at[c], (q, q * r + i)).wait_send()
+
+    @pl.when(g == q)
+    def _():
+        for k in range(1, nq):
+            rcopy(s.pblk, s.pblk, s.pb_s.at[k], s.pb_r, (rq(k), c)).wait_send()
+
+
+def halves_of(ffc):
+    return 2 if ffc % (2 * LANES) == 0 else 1
+
+
+def per_device_fast(nq, nc, hidden_in, lengths, gate_weight, up_weight, down_weight, code_weight, corpus_codes):
+    slots, w = hidden_in.shape
+    r = nc // nq
+    ng = nc // r
+    nreal = nq * slots * REAL_NUM // REAL_DEN
+    dq, ffc = gate_weight.shape
+    bm = 8 * nc
+    nblk = nreal // bm
+    nh = halves_of(ffc)
+    hw = ffc // nh
+    nu = nblk * nh
+    qm, lm, pm = bm // nq, bm // r, bm // nc
+    tb = nblk * pm
+    nqueries = nq * lengths.shape[0]
+    bits = code_weight.shape[1]
+    bw = bits // nq
+    vm, dma = pltpu.VMEM, pltpu.SemaphoreType.DMA
+    scratch = dict(
+        gate=vm(gate_weight.shape, BF16), up=vm(up_weight.shape, BF16), down=vm(down_weight.shape, BF16),
+        code=vm(code_weight.shape, BF16), corp=vm(corpus_codes.shape, BF16),
+        colbuf=vm((nq, slots, w), BF16), lens_all=vm((nq, 8, slots), jnp.int32), xall=vm((r, nblk, bm, w), BF16),
+        xn=vm((bm, dq), BF16), inv_c=vm((nblk, bm, LANES), F32),
+        st_send=vm((8, slots), F32), st_recv=vm((nc, 8, slots), F32), inv_all=vm((nq, 8, slots), F32),
+        psend=vm((nu, nq, 2, qm, hw), BF16), precv=vm((nu, 4, 2, qm, hw), BF16), pown=vm((nu, 2, qm, hw), F32),
+        hall=vm((nu, nq, qm, hw), BF16),
+        lsend=vm((nblk, r, lm, dq), BF16), lrecv=vm((nblk, r, lm, dq), BF16),
+        gsend=vm((nblk, ng, pm, dq), BF16), grecv=vm((nblk, ng, pm, dq), BF16), res=vm((tb, dq), F32),
+        t_send=vm((tb, LANES), F32), t_recv=vm((nq, tb, LANES), F32),
+        pp=vm((r, nqueries, w), F32), prc=vm((nc, nqueries, w), F32), pblk=vm((nqueries, w), BF16),
+        cpart=vm((nqueries, bw), F32), crecv=vm((nc, nqueries, bw), F32), codes=vm((nq, nqueries, bw), BF16),
+        top_q=vm((nq, nqueries, LANES), F32), top_c=vm((nc, nqueries, LANES), F32),
+        w_s=dma((5,)), l_s=dma((nq,)), l_r=dma((nq,)), a_s=dma, a_r=dma((nq,)), st_s=dma((nc,)), st_r=dma((nc,)),
+        iv_s=dma((nq,)), iv_r=dma((nq,)), ch_s=dma((2, nblk)), ch_r=dma((nblk,)), la_s=dma((r, nblk)), la_r=dma((r, nblk)),
+        p_s=dma((nu, 3)), p_r=dma((nu, 3)), h_s=dma((nu, 3)), h_r=dma((nu, 3)),
+        lr_s=dma((nblk, r)), lr_r=dma((nblk, r)), g_s=dma((nblk, ng)), g_r=dma((nblk, ng)),
+        t_s=dma((nq,)), t_r=dma((nq,)), pp_s=dma((r,)), pp_r=dma((nc,)), pb_s=dma((nq,)), pb_r=dma,
+        c_s=dma((nc,)), c_r=dma((nc,)), o_s=dma((nq,)), o_r=dma((nq,)),
+        tq_s=dma((nq,)), tq_r=dma((nq,)), tc_s=dma((nc,)), tc_r=dma((nc,)),
+    )
+    dims = (nq, nc, r, nblk, bm, nh, hw, w * nc)
+    vspec, aspec = pl.BlockSpec(memory_space=pltpu.VMEM), pl.BlockSpec(memory_space=pl.ANY)
+    sspec = pl.BlockSpec(memory_space=pltpu.SMEM)
+    return pl.pallas_call(
+        functools.partial(fast_kernel, dims, tuple(scratch)),
+        out_shape=jax.ShapeDtypeStruct((nqueries, TOPK), F32),
+        in_specs=[vspec, sspec] + [aspec] * 5,
+        out_specs=vspec,
+        scratch_shapes=list(scratch.values()),
+        compiler_params=pltpu.CompilerParams(
+            collective_id=0, has_side_effects=True, vmem_limit_bytes=60 * 1024 * 1024),
+    )(hidden_in, lengths, gate_weight, up_weight, down_weight, code_weight, corpus_codes)
+
+
+def per_device(nq, nc, hidden_in, *rest):
+    slots, w = hidden_in.shape
+    nreal = nq * slots * REAL_NUM // REAL_DEN
+    fits = nreal % (8 * nc) == 0 and w % LANES == 0
+    body = per_device_fast if fits else per_device_general
+    return body(nq, nc, hidden_in, *rest)
 
 
 def solution(mesh):

time: 111 us -> 109 us (0.982)
  local copies, waits for them, and re-layouts: 2.7 us -> 1.3 us
    broadcast_in_dim x3 -> x0, local copies, waits for them, and re-layouts: 1.41 us -> none  [per_device(): lens = jnp.broadcast_to(jnp.repeat(lengths, SEQ)[None, :], (8, slots))]
where the time goes in v1:
time: 109 us
  Pallas kernels  108 us (99%)
  local copies, waits for them, and re-layouts  1.3 us (1%)
    pallas_call x1, Pallas kernels, per_device_fast(): pl.pallas_call(functools.partial(fast_kernel, dims, tuple(scratch)), out_...  108 us

profile of v1, /device:TPU:0, one launch (start us, length us, event | category | flops | bytes accessed | tf_op | source)
XLA Modules:
  0.0 109.2 jit_solution(7647857461362419471)
XLA Ops:
  0.0 107.9 %shard_map.73 = f32[16,100]{1,0:T(8,128)} custom-call(bf16[128,512]{1,0:T(8,128)(2,1)} %hid.1, s32[4]{0:T(128)} %lens.1, bf16[1024,1792]{1,0:T(8,128)(2,1)} %gate_h.1, bf16[1024,1792]{1,0:T(8,128)(2,1)} %up_h.1, bf16[1792,1024]{1,0:T(8,128)(2,1)} %down_h.1, bf16[512,1024]{1,0:T(8,128)(2,1)} %code_h.1, bf16[512,1024]{1,0:T(8,128)(2,1)} %corp_h.1), custom_call_target="tpu_custom_call" | custom-call | tf_op jit(solution)/shard_map/pallas_call | solution.py:983
  107.9 1.3 %copy.9 = f32[16,100]{1,0:T(8,128)} copy(f32[16,100]{1,0:T(8,128)} %shard_map.73) | data formatting | bytes 12800

commit v2 on v1

--- a/solution.py
+++ b/solution.py
@@ -510,7 +510,7 @@
 
 
 def fast_kernel(dims, names, hid, lens, gate_h, up_h, down_h, code_h, corp_h, out, *refs):
-    nq, nc, r, nblk, bm, nh, hw, d_all = dims
+    nq, nc, r, nblk, bm, nh, hw, lag, d_all = dims
     s = types.SimpleNamespace(**dict(zip(names, refs)))
     q = lax.axis_index("query")
     c = lax.axis_index("corpus")
@@ -523,57 +523,69 @@
     nreal = nblk * bm
     qm, lm, pm = bm // nq, bm // r, bm // nc
     nu = nblk * nh
-    bw = s.code.shape[1] // nq
-    drains = []
-
-    loads = []
-    for i, (a, b) in enumerate(((gate_h, s.gate), (up_h, s.up), (down_h, s.down), (code_h, s.code), (corp_h, s.corp))):
-        cp = pltpu.make_async_copy(a, b, s.w_s.at[i])
-        cp.start()
-        loads.append(cp)
-
+    bw = s.codew.shape[2] // nq
+    gate, up, code, corp = s.gu.at[0], s.gu.at[1], s.codew.at[0], s.codew.at[1]
+
+    first = pltpu.make_async_copy(hid, s.colbuf.at[q], s.w_s.at[0])
+    first.start()
+    counts = pltpu.make_async_copy(lens, s.lens_s, s.w_s.at[1])
+    counts.start()
+    for a, b, k in ((gate_h, gate, 2), (up_h, up, 2), (down_h, s.down, 3), (code_h, code, 4), (corp_h, corp, 4)):
+        pltpu.make_async_copy(a, b, s.w_s.at[k]).start()
+
+    def loaded(ref, k):
+        pltpu.make_async_copy(ref, ref, s.w_s.at[k]).wait()
+
+    def rq(k):
+        return lax.rem(q + k, nq)
+
+    def rc(k):
+        return lax.rem(c + k, nc)
+
+    def lane(k):
+        return lax.rem(j + k, r)
+
+    def got(ref, sem):
+        rcopy(ref, ref, sem, sem, (rq(1), c)).wait_recv()
+
+    def sent(ref, sem):
+        rcopy(ref, ref, sem, sem, (rq(1), c)).wait_send()
+
+    def to_query(src, ref, ss, rs):
+        for k in range(1, nq):
+            rcopy(src, ref.at[q], ss, rs, (rq(k), c)).start()
+
+    def to_corpus(src, ref, ss, rs):
+        for k in range(1, nc):
+            rcopy(src, ref.at[c], ss, rs, (q, rc(k))).start()
+
+    barrier = pltpu.get_barrier_semaphore()
+    for k in range(1, nq):
+        pl.semaphore_signal(barrier, inc=1, device_id=(rq(k), c), device_id_type=pl.DeviceIdType.MESH)
+    for k in range(1, nc):
+        pl.semaphore_signal(barrier, inc=1, device_id=(q, rc(k)), device_id_type=pl.DeviceIdType.MESH)
+
+    first.wait()
+    squares = jnp.square(s.colbuf[q].astype(F32))
+    s.st_send[...] = lax.dot_general(jnp.ones((8, w), F32), squares, (((1,), (1,)), ((), ())),
+                                     precision=lax.Precision.HIGHEST, preferred_element_type=F32)
+    counts.wait()
     slot_query = lax.broadcasted_iota(jnp.int32, (8, slots), 1) // SEQ
     own_lens = jnp.zeros((8, slots), jnp.int32)
     for k in range(slots // SEQ):
-        own_lens = jnp.where(slot_query == k, lens[k], own_lens)
+        own_lens = jnp.where(slot_query == k, s.lens_s[k], own_lens)
     s.lens_all[q] = own_lens
 
-    def rq(k):
-        return lax.rem(q + k, nq)
-
-    def rc(k):
-        return lax.rem(c + k, nc)
-
-    def lane(k):
-        return lax.rem(j + k, r)
-
-    def send(cp):
-        cp.start()
-        drains.append(cp.wait_send)
-
-    barrier = pltpu.get_barrier_semaphore()
-    for k in range(1, nq):
-        pl.semaphore_signal(barrier, inc=1, device_id=(rq(k), c), device_id_type=pl.DeviceIdType.MESH)
-    for k in range(1, nc):
-        pl.semaphore_signal(barrier, inc=1, device_id=(q, rc(k)), device_id_type=pl.DeviceIdType.MESH)
     pl.semaphore_wait(barrier, nq - 1 + nc - 1)
 
-    for k in range(1, nq):
-        send(rcopy(s.lens_all.at[q], s.lens_all.at[q], s.l_s.at[k], s.l_r.at[q], (rq(k), c)))
-
     @pl.when(q != g)
     def _():
-        rcopy(hid, s.colbuf.at[q], s.a_s, s.a_r.at[q], (g, c)).start()
-
-    squares = jnp.square(hid[...].astype(F32))
-    s.st_send[...] = lax.dot_general(jnp.ones((8, w), F32), squares, (((1,), (1,)), ((), ())),
-                                     precision=lax.Precision.HIGHEST, preferred_element_type=F32)
-    for k in range(1, nc):
-        send(rcopy(s.st_send, s.st_recv.at[c], s.st_s.at[k], s.st_r.at[c], (q, rc(k))))
+        rcopy(s.colbuf.at[q], s.colbuf.at[q], s.a_s, s.a_r, (g, c)).start()
+
+    to_query(s.lens_all.at[q], s.lens_all, s.l_s, s.l_r)
+    to_corpus(s.st_send, s.st_recv, s.st_s, s.st_r)
     s.st_recv[c] = s.st_send[...]
-    for k in range(1, nq):
-        p = rq(k)
-        rcopy(s.lens_all.at[p], s.lens_all.at[p], s.l_s.at[k], s.l_r.at[p], (p, c)).wait_recv()
+    got(s.lens_all.at[pl.ds(0, nq - 1)], s.l_r)
     lens_row = jnp.concatenate([s.lens_all[i] for i in range(nq)], axis=1)
     slot = lax.broadcasted_iota(jnp.int32, (8, total), 1)
     valid = lax.rem(slot, SEQ) < lens_row
@@ -581,31 +593,24 @@
     pos = mm(valid.astype(F32).astype(BF16), before.astype(F32).astype(BF16)).astype(jnp.int32)
     pos = jnp.where(valid, pos, -1)[:1]
 
-    for k in range(1, nc):
-        p = rc(k)
-        rcopy(s.st_send, s.st_recv.at[p], s.st_s.at[k], s.st_r.at[p], (q, p)).wait_recv()
+    got(s.st_recv.at[pl.ds(0, nc - 1)], s.st_r)
     stat = s.st_recv[0]
     for i in range(1, nc):
         stat = stat + s.st_recv[i]
     s.inv_all[q] = lax.rsqrt(stat / d_all + epsilon)
-    for k in range(1, nq):
-        send(rcopy(s.inv_all.at[q], s.inv_all.at[q], s.iv_s.at[k], s.iv_r.at[q], (rq(k), c)))
+    to_query(s.inv_all.at[q], s.inv_all, s.iv_s, s.iv_r)
 
     def block(b, jj):
         return s.xall.at[jj, b]
 
     def down_chain(b):
-        return rcopy(block(b, j), block(b, j), s.ch_s.at[0, b], s.ch_r.at[b], (q, jnp.maximum(c - r, 0)))
+        return rcopy(block(b, j), block(b, j), s.ch_s.at[0], s.ch_r.at[b], (q, jnp.maximum(c - r, 0)))
 
     def up_chain(b):
-        return rcopy(block(b, j), block(b, j), s.ch_s.at[1, b], s.ch_r.at[b], (q, jnp.minimum(c + r, nc - 1)))
+        return rcopy(block(b, j), block(b, j), s.ch_s.at[1], s.ch_r.at[b], (q, jnp.minimum(c + r, nc - 1)))
 
     def side(b, k):
-        return rcopy(block(b, j), block(b, j), s.la_s.at[k, b], s.la_r.at[j, b], (q, g * r + lane(k)))
-
-    def side_in(b, k):
-        p = lane(k)
-        return rcopy(block(b, p), block(b, p), s.la_s.at[k, b], s.la_r.at[p, b], (q, g * r + p))
+        return rcopy(block(b, j), block(b, j), s.la_s, s.la_r.at[b], (q, g * r + lane(k)))
 
     sends_up = jnp.logical_and(g >= q, g < ng - 1)
     sends_down = jnp.logical_and(g <= q, g > 0)
@@ -624,10 +629,7 @@
 
     @pl.when(q == g)
     def _():
-        s.colbuf[q] = hid[...]
-        for k in range(1, nq):
-            p = rq(k)
-            rcopy(hid, s.colbuf.at[p], s.a_s, s.a_r.at[p], (p, c)).wait_recv()
+        got(s.colbuf.at[pl.ds(0, nq - 1)], s.a_r)
         stacked = s.colbuf[...].reshape(total, w)
         for b in range(nblk):
             row = lax.broadcasted_iota(jnp.int32, (bm, total), 0) + b * bm
@@ -635,17 +637,14 @@
             s.xall[j, b] = mm(pick, stacked).astype(BF16)
             pass_on(b)
 
-    for k in range(1, nq):
-        p = rq(k)
-        rcopy(s.inv_all.at[p], s.inv_all.at[p], s.iv_s.at[k], s.iv_r.at[p], (p, c)).wait_recv()
+    got(s.inv_all.at[pl.ds(0, nq - 1)], s.iv_r)
     inv_row = jnp.concatenate([s.inv_all[i] for i in range(nq)], axis=1)[:1]
     for b in range(nblk):
         row = lax.broadcasted_iota(jnp.int32, (bm, total), 0) + b * bm
         col = jnp.sum(jnp.where(pos == row, inv_row, 0.0), axis=1, keepdims=True)
         s.inv_c[b] = jnp.broadcast_to(col, (bm, LANES))
 
-    loads[0].wait()
-    loads[1].wait()
+    loaded(s.gu, 2)
 
     side_a = q + 1 - 2 * lax.rem(q, 2)
     side_b = q + 2 - 4 * (q // 2)
@@ -657,31 +656,22 @@
 
     def near_part(n):
         one, _ = sides(n)
-        return rcopy(s.psend.at[n, one], s.precv.at[n, 0], s.p_s.at[n, 0], s.p_r.at[n, 0], (one, c))
+        return rcopy(s.psend.at[n, one], s.precv.at[n, 0], s.p_s, s.p_r.at[n], (one, c))
 
     def far_part(n):
         one, _ = sides(n)
-        return rcopy(s.psend.at[n, far], s.precv.at[n, 1], s.p_s.at[n, 1], s.p_r.at[n, 1], (one, c))
+        return rcopy(s.psend.at[n, far], s.precv.at[n, 2], s.p_s, s.pf_r.at[n], (one, c))
 
     def passed_part(n):
         _, two = sides(n)
-        return rcopy(s.precv.at[n, 3], s.precv.at[n, 2], s.p_s.at[n, 2], s.p_r.at[n, 2], (two, c))
-
-    def h_near(n, k):
-        to = sides(n)[k]
-        return rcopy(s.hall.at[n, q], s.hall.at[n, q], s.h_s.at[n, k], s.h_r.at[n, k], (to, c))
-
-    def h_near_in(n, k):
-        to = sides(n)[k]
-        return rcopy(s.hall.at[n, to], s.hall.at[n, to], s.h_s.at[n, k], s.h_r.at[n, k], (to, c))
-
-    def h_pass(n):
+        return rcopy(s.precv.at[n, 3], s.precv.at[n, 1], s.p_s, s.p_r.at[n], (two, c))
+
+    def h_near(n, k, sem):
+        return rcopy(s.hall.at[n, q], s.hall.at[n, q], s.h_s, sem, (sides(n)[k], c))
+
+    def h_pass(n, sem):
         one, two = sides(n)
-        return rcopy(s.hall.at[n, one], s.hall.at[n, one], s.h_s.at[n, 2], s.h_r.at[n, 2], (two, c))
-
-    def h_pass_in(n):
-        _, two = sides(n)
-        return rcopy(s.hall.at[n, far], s.hall.at[n, far], s.h_s.at[n, 2], s.h_r.at[n, 2], (two, c))
+        return rcopy(s.hall.at[n, one], s.hall.at[n, one], s.h_s, sem, (two, c))
 
     def products(b, carry):
         @pl.when(q != g)
@@ -689,15 +679,14 @@
             up_chain(b).wait_recv()
             pass_on(b)
 
-        for k in range(1, r):
-            side_in(b, k).wait_recv()
+        got(s.xall.at[pl.ds(0, r - 1), b], s.la_r.at[b])
         scale = s.inv_c[b][:, :1]
         for i in range(r):
             s.xn[:, i * w:(i + 1) * w] = (s.xall[i, b].astype(F32) * scale).astype(BF16)
         xb = s.xn[...]
         for h in range(nh):
             n = b * nh + h
-            for e, wref in enumerate((s.gate, s.up)):
+            for e, wref in enumerate((gate, up)):
                 full = mm(xb, wref[:, h * hw:(h + 1) * hw])
                 for i in range(nq):
                     s.psend[n, i, e] = full[i * qm:(i + 1) * qm].astype(BF16)
@@ -717,60 +706,58 @@
     for i in range(r):
         s.res[:, i * w:(i + 1) * w] = mm(own_rows, s.xall[i].reshape(nreal, w))
 
-    loads[2].wait()
+    loaded(s.down, 3)
 
     def passes(n, carry):
         _, two = sides(n)
-        far_part(n).wait_recv()
-        s.precv[n, 3] = (s.psend[n, two].astype(F32) + s.precv[n, 1].astype(F32)).astype(BF16)
+        got(s.precv.at[n, 2], s.pf_r.at[n])
+        s.precv[n, 3] = (s.psend[n, two].astype(F32) + s.precv[n, 2].astype(F32)).astype(BF16)
         passed_part(n).start()
         return carry
 
     def reduce_unit(n):
-        near_part(n).wait_recv()
-        passed_part(n).wait_recv()
-        gsum = s.pown[n, 0] + s.precv[n, 0, 0].astype(F32) + s.precv[n, 2, 0].astype(F32)
-        usum = s.pown[n, 1] + s.precv[n, 0, 1].astype(F32) + s.precv[n, 2, 1].astype(F32)
+        got(s.precv.at[n, pl.ds(0, 2)], s.p_r.at[n])
+        gsum = s.pown[n, 0] + s.precv[n, 0, 0].astype(F32) + s.precv[n, 1, 0].astype(F32)
+        usum = s.pown[n, 1] + s.precv[n, 0, 1].astype(F32) + s.precv[n, 1, 1].astype(F32)
         s.hall[n, q] = (gsum / (1.0 + jnp.exp(-gsum)) * usum).astype(BF16)
-        h_near(n, 0).start()
-        h_near(n, 1).start()
+        h_near(n, 0, s.hn_r.at[n]).start()
+        h_near(n, 1, s.hb_r.at[n // nh]).start()
 
     def relay_unit(n):
-        h_near_in(n, 0).wait_recv()
-        h_pass(n).start()
+        got(s.hall.at[n, 0], s.hn_r.at[n])
+        h_pass(n, s.hb_r.at[n // nh]).start()
 
     def reduces(n, carry):
         reduce_unit(n)
-        relay_unit(n - 1)
+        return carry
+
+    def reduces_relays(n, carry):
+        reduce_unit(n)
+        relay_unit(n - lag)
+        return carry
+
+    def relays(n, carry):
+        relay_unit(n)
         return carry
 
     lax.fori_loop(0, nu, passes, 0)
-    reduce_unit(0)
-    lax.fori_loop(1, nu, reduces, 0)
-    relay_unit(nu - 1)
+    lax.fori_loop(0, lag, reduces, 0)
+    lax.fori_loop(lag, nu, reduces_relays, 0)
+    lax.fori_loop(nu - lag, nu, relays, 0)
 
     def lane_send(b, k):
         t = lane(k)
-        return rcopy(s.lsend.at[b, t], s.lrecv.at[b, j], s.lr_s.at[b, k], s.lr_r.at[b, j], (q, g * r + t))
-
-    def lane_in(b, k):
-        p = lane(k)
-        return rcopy(s.lsend.at[b, p], s.lrecv.at[b, p], s.lr_s.at[b, k], s.lr_r.at[b, p], (q, g * r + p))
+        return rcopy(s.lsend.at[b, t], s.lrecv.at[b, j], s.lr_s, s.lr_r.at[b], (q, g * r + t))
 
     def group_send(b, k):
         t = lax.rem(g + k, ng)
-        return rcopy(s.gsend.at[b, t], s.grecv.at[b, g], s.g_s.at[b, k], s.g_r.at[b, g], (q, t * r + j))
-
-    def group_in(b, k):
-        p = lax.rem(g + k, ng)
-        return rcopy(s.gsend.at[b, p], s.grecv.at[b, p], s.g_s.at[b, k], s.g_r.at[b, p], (q, p * r + j))
+        return rcopy(s.gsend.at[b, t], s.grecv.at[b, g], s.g_s, s.g_r.at[b], (q, t * r + j))
 
     def down_block(b):
         part = None
+        got(s.hall.at[pl.ds(b * nh, nh), pl.ds(0, 2)], s.hb_r.at[b])
         for h in range(nh):
             n = b * nh + h
-            h_near_in(n, 1).wait_recv()
-            h_pass_in(n).wait_recv()
             term = mm(s.hall[n].reshape(bm, hw), s.down[h * hw:(h + 1) * hw, :])
             part = term if part is None else part + term
         for t in range(r):
@@ -780,8 +767,8 @@
 
     def sum_block(b):
         mine = s.lsend[b, j].astype(F32)
+        got(s.lrecv.at[b, pl.ds(0, r - 1)], s.lr_r.at[b])
         for k in range(1, r):
-            lane_in(b, k).wait_recv()
             mine = mine + s.lrecv[b, lane(k)].astype(F32)
         for t in range(ng):
             s.gsend[b, t] = mine[t * pm:(t + 1) * pm].astype(BF16)
@@ -798,16 +785,15 @@
     sum_block(nblk - 1)
     for b in range(nblk):
         total_b = s.gsend[b, g].astype(F32)
+        got(s.grecv.at[b, pl.ds(0, ng - 1)], s.g_r.at[b])
         for k in range(1, ng):
-            group_in(b, k).wait_recv()
             total_b = total_b + s.grecv[b, lax.rem(g + k, ng)].astype(F32)
         s.res[b * pm:(b + 1) * pm, :] = s.res[b * pm:(b + 1) * pm, :] + total_b
     residual = s.res[...]
     tb = nblk * pm
 
     s.t_send[...] = jnp.broadcast_to(jnp.sum(residual * residual, axis=1, keepdims=True), (tb, LANES))
-    for k in range(1, nq):
-        send(rcopy(s.t_send, s.t_recv.at[q], s.t_s.at[k], s.t_r.at[q], (rq(k), c)))
+    to_query(s.t_send, s.t_recv, s.t_s, s.t_r)
     qrow = lax.broadcasted_iota(jnp.int32, (nqueries, total), 0)
     qslot = lax.broadcasted_iota(jnp.int32, (nqueries, total), 1)
     lens_b = jnp.broadcast_to(lens_row[:1], (nqueries, total)).astype(F32)
@@ -818,10 +804,9 @@
     prow = ((prow // pm) * bm + (j * ng + g) * pm + lax.rem(prow, pm)).astype(F32)
     member = jnp.where(jnp.logical_and(prow >= off_col, prow < off_col + len_col), 1.0, 0.0)
     tsum = s.t_send[...]
-    for k in range(1, nq):
-        p = rq(k)
-        rcopy(s.t_send, s.t_recv.at[p], s.t_s.at[k], s.t_r.at[p], (p, c)).wait_recv()
-        tsum = tsum + s.t_recv[p]
+    got(s.t_recv.at[pl.ds(0, nq - 1)], s.t_r)
+    for k in range(1, nq):
+        tsum = tsum + s.t_recv[rq(k)]
     final = residual * lax.rsqrt(tsum[:, :1] / d_all + epsilon)
     pooled_part = mm(member, final, lax.Precision.HIGHEST)
     for i in range(r):
@@ -829,109 +814,87 @@
     for i in range(r):
         @pl.when(c != q * r + i)
         def _(i=i):
-            rcopy(s.pp.at[i], s.prc.at[c], s.pp_s.at[i], s.pp_r.at[c], (q, q * r + i)).start()
+            rcopy(s.pp.at[i], s.prc.at[c], s.pp_s, s.pp_r, (q, q * r + i)).start()
 
     @pl.when(g == q)
     def _():
         pooled = s.pp[j]
+        got(s.prc.at[pl.ds(0, nc - 1)], s.pp_r)
         for k in range(1, nc):
-            p = rc(k)
-            rcopy(s.pp.at[j], s.prc.at[p], s.pp_s.at[0], s.pp_r.at[p], (q, p)).wait_recv()
-            pooled = pooled + s.prc[p]
-        s.pblk[...] = (pooled / len_col).astype(BF16)
+            pooled = pooled + s.prc[rc(k)]
+        s.pblk[0] = (pooled / len_col).astype(BF16)
         for k in range(1, nq):
-            rcopy(s.pblk, s.pblk, s.pb_s.at[k], s.pb_r, (rq(k), c)).start()
-
-    loads[3].wait()
-    loads[4].wait()
+            rcopy(s.pblk.at[0], s.pblk.at[0], s.pb_s, s.pb_r, (rq(k), c)).start()
+
+    loaded(s.codew, 4)
 
     @pl.when(g != q)
     def _():
-        rcopy(s.pblk, s.pblk, s.pb_s.at[0], s.pb_r, (g, c)).wait_recv()
-
-    s.cpart[...] = mm(s.pblk[...], s.code[:, pl.ds(pl.multiple_of(q * bw, bw), bw)])
-    for k in range(1, nc):
-        send(rcopy(s.cpart, s.crecv.at[c], s.c_s.at[k], s.c_r.at[c], (q, rc(k))))
+        got(s.pblk.at[0], s.pb_r)
+
+    s.cpart[...] = mm(s.pblk[0], code[:, pl.ds(pl.multiple_of(q * bw, bw), bw)])
+    to_corpus(s.cpart, s.crecv, s.c_s, s.c_r)
     s.crecv[c] = s.cpart[...]
-    for k in range(1, nc):
-        p = rc(k)
-        rcopy(s.cpart, s.crecv.at[p], s.c_s.at[k], s.c_r.at[p], (q, p)).wait_recv()
+    got(s.crecv.at[pl.ds(0, nc - 1)], s.c_r)
     csum = s.crecv[0]
     for i in range(1, nc):
         csum = csum + s.crecv[i]
     s.codes[q] = csum.astype(BF16)
-    for k in range(1, nq):
-        send(rcopy(s.codes.at[q], s.codes.at[q], s.o_s.at[k], s.o_r.at[q], (rq(k), c)))
-    for k in range(1, nq):
-        p = rq(k)
-        rcopy(s.codes.at[p], s.codes.at[p], s.o_s.at[k], s.o_r.at[p], (p, c)).wait_recv()
+    to_query(s.codes.at[q], s.codes, s.o_s, s.o_r)
+    got(s.codes.at[pl.ds(0, nq - 1)], s.o_r)
     qcodes = jnp.concatenate([s.codes[i] for i in range(nq)], axis=1)
-    scale = 1.0 / math.sqrt(s.corp.shape[1])
-    scores = lax.dot_general(qcodes, s.corp[...], (((1,), (1,)), ((), ())), preferred_element_type=F32) * scale
-
-    blocks = s.corp.shape[0] // LANES
+    scale = 1.0 / math.sqrt(corp.shape[1])
+    scores = lax.dot_general(qcodes, corp[...], (((1,), (1,)), ((), ())), preferred_element_type=F32) * scale
+
+    blocks = corp.shape[0] // LANES
     lists = jnp.concatenate([scores[:, i * LANES:(i + 1) * LANES] for i in range(blocks)], axis=0)
     best = merge_all(sort_lanes(lists), nqueries, q >= nq // 2)
     s.top_q[q] = best
-    for k in range(1, nq):
-        send(rcopy(s.top_q.at[q], s.top_q.at[q], s.tq_s.at[k], s.tq_r.at[q], (rq(k), c)))
-    for k in range(1, nq):
-        p = rq(k)
-        rcopy(s.top_q.at[p], s.top_q.at[p], s.tq_s.at[k], s.tq_r.at[p], (p, c)).wait_recv()
+    to_query(s.top_q.at[q], s.top_q, s.tq_s, s.tq_r)
+    got(s.top_q.at[pl.ds(0, nq - 1)], s.tq_r)
     best = merge_all(s.top_q[...].reshape(nq * nqueries, LANES), nqueries, c >= nc // 2)
     s.top_c[c] = best
-    for k in range(1, nc):
-        send(rcopy(s.top_c.at[c], s.top_c.at[c], s.tc_s.at[k], s.tc_r.at[c], (q, rc(k))))
-    for k in range(1, nc):
-        p = rc(k)
-        rcopy(s.top_c.at[p], s.top_c.at[p], s.tc_s.at[k], s.tc_r.at[p], (q, p)).wait_recv()
+    to_corpus(s.top_c.at[c], s.top_c, s.tc_s, s.tc_r)
+    got(s.top_c.at[pl.ds(0, nc - 1)], s.tc_r)
     best = merge_all(s.top_c[...].reshape(nc * nqueries, LANES), nqueries, False)
     out[...] = best[:, :TOPK]
 
-    for wait in drains:
-        wait()
+    sent(s.lens_all.at[pl.ds(0, nq - 1)], s.l_s)
+    sent(s.st_recv.at[pl.ds(0, nc - 1)], s.st_s)
+    sent(s.inv_all.at[pl.ds(0, nq - 1)], s.iv_s)
 
     @pl.when(q != g)
     def _():
-        rcopy(hid, s.colbuf.at[q], s.a_s, s.a_r.at[q], (g, c)).wait_send()
-
-    def drain_blocks(b, carry):
-        @pl.when(sends_up)
-        def _():
-            up_chain(b).wait_send()
-
-        @pl.when(sends_down)
-        def _():
-            down_chain(b).wait_send()
-
-        for k in range(1, r):
-            side(b, k).wait_send()
-        for k in range(1, r):
-            lane_send(b, k).wait_send()
-        for k in range(1, ng):
-            group_send(b, k).wait_send()
-        return carry
-
-    def drain_units(n, carry):
-        far_part(n).wait_send()
-        near_part(n).wait_send()
-        passed_part(n).wait_send()
-        h_near(n, 0).wait_send()
-        h_near(n, 1).wait_send()
-        h_pass(n).wait_send()
-        return carry
-
-    lax.fori_loop(0, nblk, drain_blocks, 0)
-    lax.fori_loop(0, nu, drain_units, 0)
-    for i in range(r):
-        @pl.when(c != q * r + i)
-        def _(i=i):
-            rcopy(s.pp.at[i], s.prc.at[c], s.pp_s.at[i], s.pp_r.at[c], (q, q * r + i)).wait_send()
+        sent(s.colbuf.at[0], s.a_s)
+
+    @pl.when(sends_down)
+    def _():
+        sent(s.xall.at[0], s.ch_s.at[0])
+
+    @pl.when(sends_up)
+    def _():
+        sent(s.xall.at[0], s.ch_s.at[1])
+
+    sent(s.xall.at[pl.ds(0, r - 1)], s.la_s)
+    sent(s.psend.at[:, pl.ds(0, 3)], s.p_s)
+    sent(s.hall.at[:, pl.ds(0, 3)], s.h_s)
+    sent(s.lsend.at[:, pl.ds(0, r - 1)], s.lr_s)
+    sent(s.gsend.at[:, pl.ds(0, ng - 1)], s.g_s)
+    sent(s.t_recv.at[pl.ds(0, nq - 1)], s.t_s)
 
     @pl.when(g == q)
     def _():
-        for k in range(1, nq):
-            rcopy(s.pblk, s.pblk, s.pb_s.at[k], s.pb_r, (rq(k), c)).wait_send()
+        sent(s.pp.at[pl.ds(0, r - 1)], s.pp_s)
+        sent(s.pblk.at[pl.ds(0, nq - 1)], s.pb_s)
+
+    @pl.when(g != q)
+    def _():
+        sent(s.pp, s.pp_s)
+
+    sent(s.crecv.at[pl.ds(0, nc - 1)], s.c_s)
+    sent(s.codes.at[pl.ds(0, nq - 1)], s.o_s)
+    sent(s.top_q.at[pl.ds(0, nq - 1)], s.tq_s)
+    sent(s.top_c.at[pl.ds(0, nc - 1)], s.tc_s)
 
 
 def halves_of(ffc):
@@ -956,8 +919,8 @@
     bw = bits // nq
     vm, dma = pltpu.VMEM, pltpu.SemaphoreType.DMA
     scratch = dict(
-        gate=vm(gate_weight.shape, BF16), up=vm(up_weight.shape, BF16), down=vm(down_weight.shape, BF16),
-        code=vm(code_weight.shape, BF16), corp=vm(corpus_codes.shape, BF16),
+        gu=vm((2,) + gate_weight.shape, BF16), down=vm(down_weight.shape, BF16), codew=vm((2,) + code_weight.shape, BF16),
+        lens_s=pltpu.SMEM(lengths.shape, jnp.int32),
         colbuf=vm((nq, slots, w), BF16), lens_all=vm((nq, 8, slots), jnp.int32), xall=vm((r, nblk, bm, w), BF16),
         xn=vm((bm, dq), BF16), inv_c=vm((nblk, bm, LANES), F32),
         st_send=vm((8, slots), F32), st_recv=vm((nc, 8, slots), F32), inv_all=vm((nq, 8, slots), F32),
@@ -966,24 +929,22 @@
         lsend=vm((nblk, r, lm, dq), BF16), lrecv=vm((nblk, r, lm, dq), BF16),
         gsend=vm((nblk, ng, pm, dq), BF16), grecv=vm((nblk, ng, pm, dq), BF16), res=vm((tb, dq), F32),
         t_send=vm((tb, LANES), F32), t_recv=vm((nq, tb, LANES), F32),
-        pp=vm((r, nqueries, w), F32), prc=vm((nc, nqueries, w), F32), pblk=vm((nqueries, w), BF16),
+        pp=vm((r, nqueries, w), F32), prc=vm((nc, nqueries, w), F32), pblk=vm((nq, nqueries, w), BF16),
         cpart=vm((nqueries, bw), F32), crecv=vm((nc, nqueries, bw), F32), codes=vm((nq, nqueries, bw), BF16),
         top_q=vm((nq, nqueries, LANES), F32), top_c=vm((nc, nqueries, LANES), F32),
-        w_s=dma((5,)), l_s=dma((nq,)), l_r=dma((nq,)), a_s=dma, a_r=dma((nq,)), st_s=dma((nc,)), st_r=dma((nc,)),
-        iv_s=dma((nq,)), iv_r=dma((nq,)), ch_s=dma((2, nblk)), ch_r=dma((nblk,)), la_s=dma((r, nblk)), la_r=dma((r, nblk)),
-        p_s=dma((nu, 3)), p_r=dma((nu, 3)), h_s=dma((nu, 3)), h_r=dma((nu, 3)),
-        lr_s=dma((nblk, r)), lr_r=dma((nblk, r)), g_s=dma((nblk, ng)), g_r=dma((nblk, ng)),
-        t_s=dma((nq,)), t_r=dma((nq,)), pp_s=dma((r,)), pp_r=dma((nc,)), pb_s=dma((nq,)), pb_r=dma,
-        c_s=dma((nc,)), c_r=dma((nc,)), o_s=dma((nq,)), o_r=dma((nq,)),
-        tq_s=dma((nq,)), tq_r=dma((nq,)), tc_s=dma((nc,)), tc_r=dma((nc,)),
+        w_s=dma((5,)), l_s=dma, l_r=dma, a_s=dma, a_r=dma, st_s=dma, st_r=dma, iv_s=dma, iv_r=dma,
+        ch_s=dma((2,)), ch_r=dma((nblk,)), la_s=dma, la_r=dma((nblk,)),
+        p_s=dma, p_r=dma((nu,)), pf_r=dma((nu,)), h_s=dma, hn_r=dma((nu,)), hb_r=dma((nblk,)),
+        lr_s=dma, lr_r=dma((nblk,)), g_s=dma, g_r=dma((nblk,)),
+        t_s=dma, t_r=dma, pp_s=dma, pp_r=dma, pb_s=dma, pb_r=dma, c_s=dma, c_r=dma, o_s=dma, o_r=dma,
+        tq_s=dma, tq_r=dma, tc_s=dma, tc_r=dma,
     )
-    dims = (nq, nc, r, nblk, bm, nh, hw, w * nc)
+    dims = (nq, nc, r, nblk, bm, nh, hw, min(3, nu - 1), w * nc)
     vspec, aspec = pl.BlockSpec(memory_space=pltpu.VMEM), pl.BlockSpec(memory_space=pl.ANY)
-    sspec = pl.BlockSpec(memory_space=pltpu.SMEM)
     return pl.pallas_call(
         functools.partial(fast_kernel, dims, tuple(scratch)),
         out_shape=jax.ShapeDtypeStruct((nqueries, TOPK), F32),
-        in_specs=[vspec, sspec] + [aspec] * 5,
+        in_specs=[aspec] * 7,
         out_specs=vspec,
         scratch_shapes=list(scratch.values()),
         compiler_params=pltpu.CompilerParams(
@@ -994,7 +955,7 @@
 def per_device(nq, nc, hidden_in, *rest):
     slots, w = hidden_in.shape
     nreal = nq * slots * REAL_NUM // REAL_DEN
-    fits = nreal % (8 * nc) == 0 and w % LANES == 0
+    fits = nreal % (8 * nc) == 0 and w % LANES == 0 and rest[4].shape == rest[5].shape
     body = per_device_fast if fits else per_device_general
     return body(nq, nc, hidden_in, *rest)
 

time: 109 us -> 101 us (0.927)
  Pallas kernels: 108 us -> 99.4 us
    pallas_call x1, Pallas kernels: 108 us -> 99.4 us  [per_device_fast(): pl.pallas_call(functools.partial(fast_kernel, dims, tuple(scratch)), out_...]
where the time goes in v2:
time: 101 us
  Pallas kernels  99.4 us (98%)
  local copies, waits for them, and re-layouts  1.3 us (1%)
    pallas_call x1, Pallas kernels, per_device_fast(): pl.pallas_call(functools.partial(fast_kernel, dims, tuple(scratch)), out_...  99.4 us

profile of v2, /device:TPU:0, one launch (start us, length us, event | category | flops | bytes accessed | tf_op | source)
XLA Modules:
  0.0 100.7 jit_solution(10646459365845425684)
XLA Ops:
  0.0 99.4 %shard_map.73 = f32[16,100]{1,0:T(8,128)} custom-call(bf16[128,512]{1,0:T(8,128)(2,1)} %hid.1, s32[4]{0:T(128)} %lens.1, bf16[1024,1792]{1,0:T(8,128)(2,1)} %gate_h.1, bf16[1024,1792]{1,0:T(8,128)(2,1)} %up_h.1, bf16[1792,1024]{1,0:T(8,128)(2,1)} %down_h.1, bf16[512,1024]{1,0:T(8,128)(2,1)} %code_h.1, bf16[512,1024]{1,0:T(8,128)(2,1)} %corp_h.1), custom_call_target="tpu_custom_call" | custom-call | tf_op jit(solution)/shard_map/pallas_call | solution.py:944
  99.4 1.3 %copy.9 = f32[16,100]{1,0:T(8,128)} copy(f32[16,100]{1,0:T(8,128)} %shard_map.73) | data formatting | bytes 12800

commit v3 on v2

--- a/solution.py
+++ b/solution.py
@@ -510,7 +510,7 @@
 
 
 def fast_kernel(dims, names, hid, lens, gate_h, up_h, down_h, code_h, corp_h, out, *refs):
-    nq, nc, r, nblk, bm, nh, hw, lag, d_all = dims
+    nq, nc, r, nblk, bm, pr, nh, hw, d_all = dims
     s = types.SimpleNamespace(**dict(zip(names, refs)))
     q = lax.axis_index("query")
     c = lax.axis_index("corpus")
@@ -578,9 +578,21 @@
 
     pl.semaphore_wait(barrier, nq - 1 + nc - 1)
 
-    @pl.when(q != g)
+    side_a = q + 1 - 2 * lax.rem(q, 2)
+    side_b = q + 2 - 4 * (q // 2)
+    far = nq - 1 - q
+    opposite = nq - 1 - g
+    helper = g + 1 - 2 * lax.rem(g, 2)
+    upper, lower = pl.ds(0, slots // 2), pl.ds(slots // 2, slots // 2)
+
+    @pl.when(jnp.logical_and(q != g, q != opposite))
     def _():
         rcopy(s.colbuf.at[q], s.colbuf.at[q], s.a_s, s.a_r, (g, c)).start()
+
+    @pl.when(q == opposite)
+    def _():
+        rcopy(s.colbuf.at[q, lower], s.colbuf.at[q, lower], s.a_s, s.ah_r, (helper, c)).start()
+        rcopy(s.colbuf.at[q, upper], s.colbuf.at[q, upper], s.a_s, s.a_r, (g, c)).start()
 
     to_query(s.lens_all.at[q], s.lens_all, s.l_s, s.l_r)
     to_corpus(s.st_send, s.st_recv, s.st_s, s.st_r)
@@ -593,6 +605,11 @@
     pos = mm(valid.astype(F32).astype(BF16), before.astype(F32).astype(BF16)).astype(jnp.int32)
     pos = jnp.where(valid, pos, -1)[:1]
 
+    @pl.when(q == helper)
+    def _():
+        got(s.colbuf.at[0, lower], s.ah_r)
+        rcopy(s.colbuf.at[opposite, lower], s.colbuf.at[opposite, lower], s.ah_s, s.a_r, (g, c)).start()
+
     got(s.st_recv.at[pl.ds(0, nc - 1)], s.st_r)
     stat = s.st_recv[0]
     for i in range(1, nc):
@@ -600,32 +617,32 @@
     s.inv_all[q] = lax.rsqrt(stat / d_all + epsilon)
     to_query(s.inv_all.at[q], s.inv_all, s.iv_s, s.iv_r)
 
-    def block(b, jj):
-        return s.xall.at[jj, b]
-
-    def down_chain(b):
-        return rcopy(block(b, j), block(b, j), s.ch_s.at[0], s.ch_r.at[b], (q, jnp.maximum(c - r, 0)))
-
-    def up_chain(b):
-        return rcopy(block(b, j), block(b, j), s.ch_s.at[1], s.ch_r.at[b], (q, jnp.minimum(c + r, nc - 1)))
-
-    def side(b, k):
-        return rcopy(block(b, j), block(b, j), s.la_s, s.la_r.at[b], (q, g * r + lane(k)))
+    def piece(b, p):
+        return s.xall.at[j, b, pl.ds(p * pr, pr)]
+
+    def down_chain(b, p):
+        return rcopy(piece(b, p), piece(b, p), s.ch_s.at[0], s.ch_r.at[b, p], (q, jnp.maximum(c - r, 0)))
+
+    def up_chain(b, p):
+        return rcopy(piece(b, p), piece(b, p), s.ch_s.at[1], s.ch_r.at[b, p], (q, jnp.minimum(c + r, nc - 1)))
+
+    def side(b, p, k):
+        return rcopy(piece(b, p), piece(b, p), s.la_s, s.la_r.at[b], (q, g * r + lane(k)))
 
     sends_up = jnp.logical_and(g >= q, g < ng - 1)
     sends_down = jnp.logical_and(g <= q, g > 0)
 
-    def pass_on(b):
+    def pass_on(b, p):
         @pl.when(sends_up)
         def _():
-            up_chain(b).start()
+            up_chain(b, p).start()
 
         @pl.when(sends_down)
         def _():
-            down_chain(b).start()
+            down_chain(b, p).start()
 
         for k in range(1, r):
-            side(b, k).start()
+            side(b, p, k).start()
 
     @pl.when(q == g)
     def _():
@@ -635,7 +652,8 @@
             row = lax.broadcasted_iota(jnp.int32, (bm, total), 0) + b * bm
             pick = (pos == row).astype(F32).astype(BF16)
             s.xall[j, b] = mm(pick, stacked).astype(BF16)
-            pass_on(b)
+            for p in range(bm // pr):
+                pass_on(b, p)
 
     got(s.inv_all.at[pl.ds(0, nq - 1)], s.iv_r)
     inv_row = jnp.concatenate([s.inv_all[i] for i in range(nq)], axis=1)[:1]
@@ -646,10 +664,6 @@
 
     loaded(s.gu, 2)
 
-    side_a = q + 1 - 2 * lax.rem(q, 2)
-    side_b = q + 2 - 4 * (q // 2)
-    far = nq - 1 - q
-
     def sides(n):
         odd = lax.rem(n, 2)
         return side_a + (side_b - side_a) * odd, side_b + (side_a - side_b) * odd
@@ -673,11 +687,12 @@
         one, two = sides(n)
         return rcopy(s.hall.at[n, one], s.hall.at[n, one], s.h_s, sem, (two, c))
 
-    def products(b, carry):
+    def products(b):
         @pl.when(q != g)
         def _():
-            up_chain(b).wait_recv()
-            pass_on(b)
+            for p in range(bm // pr):
+                up_chain(b, p).wait_recv()
+                pass_on(b, p)
 
         got(s.xall.at[pl.ds(0, r - 1), b], s.la_r.at[b])
         scale = s.inv_c[b][:, :1]
@@ -688,32 +703,19 @@
             n = b * nh + h
             for e, wref in enumerate((gate, up)):
                 full = mm(xb, wref[:, h * hw:(h + 1) * hw])
+                s.full[h, e] = full
                 for i in range(nq):
                     s.psend[n, i, e] = full[i * qm:(i + 1) * qm].astype(BF16)
-
-                    @pl.when(q == i)
-                    def _(i=i, e=e, full=full, n=n):
-                        s.pown[n, e] = full[i * qm:(i + 1) * qm]
             far_part(n).start()
             near_part(n).start()
-        return carry
-
-    lax.fori_loop(0, nblk, products, 0)
-
-    row = lax.broadcasted_iota(jnp.int32, (nblk * pm, nreal), 0)
-    row = (row // pm) * bm + (j * ng + g) * pm + lax.rem(row, pm)
-    own_rows = (lax.broadcasted_iota(jnp.int32, (nblk * pm, nreal), 1) == row).astype(F32).astype(BF16)
-    for i in range(r):
-        s.res[:, i * w:(i + 1) * w] = mm(own_rows, s.xall[i].reshape(nreal, w))
-
-    loaded(s.down, 3)
-
-    def passes(n, carry):
+            for e in range(2):
+                s.pown[n, e] = s.full[h, e, pl.ds(pl.multiple_of(q * qm, qm), qm)]
+
+    def pass_unit(n):
         _, two = sides(n)
         got(s.precv.at[n, 2], s.pf_r.at[n])
         s.precv[n, 3] = (s.psend[n, two].astype(F32) + s.precv[n, 2].astype(F32)).astype(BF16)
         passed_part(n).start()
-        return carry
 
     def reduce_unit(n):
         got(s.precv.at[n, pl.ds(0, 2)], s.p_r.at[n])
@@ -726,24 +728,6 @@
     def relay_unit(n):
         got(s.hall.at[n, 0], s.hn_r.at[n])
         h_pass(n, s.hb_r.at[n // nh]).start()
-
-    def reduces(n, carry):
-        reduce_unit(n)
-        return carry
-
-    def reduces_relays(n, carry):
-        reduce_unit(n)
-        relay_unit(n - lag)
-        return carry
-
-    def relays(n, carry):
-        relay_unit(n)
-        return carry
-
-    lax.fori_loop(0, nu, passes, 0)
-    lax.fori_loop(0, lag, reduces, 0)
-    lax.fori_loop(lag, nu, reduces_relays, 0)
-    lax.fori_loop(nu - lag, nu, relays, 0)
 
     def lane_send(b, k):
         t = lane(k)
@@ -775,14 +759,29 @@
         for k in range(1, ng):
             group_send(b, k).start()
 
-    def downs(b, carry):
-        down_block(b)
-        sum_block(b - 1)
+    def units(unit, b):
+        for h in range(nh):
+            unit(b * nh + h)
+
+    stages = (products, functools.partial(units, pass_unit), functools.partial(units, reduce_unit),
+              functools.partial(units, relay_unit), down_block, sum_block)
+    delays = (0,1,3,4,6,7)
+
+    def turn(t, carry):
+        for stage, delay in zip(stages, delays):
+            @pl.when(jnp.logical_and(t >= delay, t < nblk + delay))
+            def _(stage=stage, delay=delay):
+                stage(t - delay)
         return carry
 
-    down_block(0)
-    lax.fori_loop(1, nblk, downs, 0)
-    sum_block(nblk - 1)
+    loaded(s.down, 3)
+    lax.fori_loop(0, nblk + delays[-1], turn, 0)
+    row = lax.broadcasted_iota(jnp.int32, (nblk * pm, nreal), 0)
+    row = (row // pm) * bm + (j * ng + g) * pm + lax.rem(row, pm)
+    own_rows = (lax.broadcasted_iota(jnp.int32, (nblk * pm, nreal), 1) == row).astype(F32).astype(BF16)
+    for i in range(r):
+        s.res[:, i * w:(i + 1) * w] = mm(own_rows, s.xall[i].reshape(nreal, w))
+
     for b in range(nblk):
         total_b = s.gsend[b, g].astype(F32)
         got(s.grecv.at[b, pl.ds(0, ng - 1)], s.g_r.at[b])
@@ -810,7 +809,7 @@
     final = residual * lax.rsqrt(tsum[:, :1] / d_all + epsilon)
     pooled_part = mm(member, final, lax.Precision.HIGHEST)
     for i in range(r):
-        s.pp[i] = pooled_part[:, i * w:(i + 1) * w]
+        s.pp[i] = pooled_part[:, i * w:(i + 1) * w].astype(BF16)
     for i in range(r):
         @pl.when(c != q * r + i)
         def _(i=i):
@@ -818,10 +817,10 @@
 
     @pl.when(g == q)
     def _():
-        pooled = s.pp[j]
+        pooled = s.pp[j].astype(F32)
         got(s.prc.at[pl.ds(0, nc - 1)], s.pp_r)
         for k in range(1, nc):
-            pooled = pooled + s.prc[rc(k)]
+            pooled = pooled + s.prc[rc(k)].astype(F32)
         s.pblk[0] = (pooled / len_col).astype(BF16)
         for k in range(1, nq):
             rcopy(s.pblk.at[0], s.pblk.at[0], s.pb_s, s.pb_r, (rq(k), c)).start()
@@ -832,13 +831,13 @@
     def _():
         got(s.pblk.at[0], s.pb_r)
 
-    s.cpart[...] = mm(s.pblk[0], code[:, pl.ds(pl.multiple_of(q * bw, bw), bw)])
+    s.cpart[...] = mm(s.pblk[0], code[:, pl.ds(pl.multiple_of(q * bw, bw), bw)]).astype(BF16)
     to_corpus(s.cpart, s.crecv, s.c_s, s.c_r)
     s.crecv[c] = s.cpart[...]
     got(s.crecv.at[pl.ds(0, nc - 1)], s.c_r)
-    csum = s.crecv[0]
+    csum = s.crecv[0].astype(F32)
     for i in range(1, nc):
-        csum = csum + s.crecv[i]
+        csum = csum + s.crecv[i].astype(F32)
     s.codes[q] = csum.astype(BF16)
     to_query(s.codes.at[q], s.codes, s.o_s, s.o_r)
     got(s.codes.at[pl.ds(0, nq - 1)], s.o_r)
@@ -867,6 +866,10 @@
     def _():
         sent(s.colbuf.at[0], s.a_s)
 
+    @pl.when(q == helper)
+    def _():
+        sent(s.colbuf.at[0, lower], s.ah_s)
+
     @pl.when(sends_down)
     def _():
         sent(s.xall.at[0], s.ch_s.at[0])
@@ -909,6 +912,7 @@
     dq, ffc = gate_weight.shape
     bm = 8 * nc
     nblk = nreal // bm
+    pr = PIECE if bm % PIECE == 0 else bm
     nh = halves_of(ffc)
     hw = ffc // nh
     nu = nblk * nh
@@ -924,22 +928,22 @@
         colbuf=vm((nq, slots, w), BF16), lens_all=vm((nq, 8, slots), jnp.int32), xall=vm((r, nblk, bm, w), BF16),
         xn=vm((bm, dq), BF16), inv_c=vm((nblk, bm, LANES), F32),
         st_send=vm((8, slots), F32), st_recv=vm((nc, 8, slots), F32), inv_all=vm((nq, 8, slots), F32),
-        psend=vm((nu, nq, 2, qm, hw), BF16), precv=vm((nu, 4, 2, qm, hw), BF16), pown=vm((nu, 2, qm, hw), F32),
+        psend=vm((nu, nq, 2, qm, hw), BF16), precv=vm((nu, 4, 2, qm, hw), BF16), pown=vm((nu, 2, qm, hw), F32), full=vm((nh, 2, bm, hw), F32),
         hall=vm((nu, nq, qm, hw), BF16),
         lsend=vm((nblk, r, lm, dq), BF16), lrecv=vm((nblk, r, lm, dq), BF16),
         gsend=vm((nblk, ng, pm, dq), BF16), grecv=vm((nblk, ng, pm, dq), BF16), res=vm((tb, dq), F32),
         t_send=vm((tb, LANES), F32), t_recv=vm((nq, tb, LANES), F32),
-        pp=vm((r, nqueries, w), F32), prc=vm((nc, nqueries, w), F32), pblk=vm((nq, nqueries, w), BF16),
-        cpart=vm((nqueries, bw), F32), crecv=vm((nc, nqueries, bw), F32), codes=vm((nq, nqueries, bw), BF16),
+        pp=vm((r, nqueries, w), BF16), prc=vm((nc, nqueries, w), BF16), pblk=vm((nq, nqueries, w), BF16),
+        cpart=vm((nqueries, bw), BF16), crecv=vm((nc, nqueries, bw), BF16), codes=vm((nq, nqueries, bw), BF16),
         top_q=vm((nq, nqueries, LANES), F32), top_c=vm((nc, nqueries, LANES), F32),
-        w_s=dma((5,)), l_s=dma, l_r=dma, a_s=dma, a_r=dma, st_s=dma, st_r=dma, iv_s=dma, iv_r=dma,
-        ch_s=dma((2,)), ch_r=dma((nblk,)), la_s=dma, la_r=dma((nblk,)),
+        w_s=dma((5,)), l_s=dma, l_r=dma, a_s=dma, a_r=dma, ah_s=dma, ah_r=dma, st_s=dma, st_r=dma, iv_s=dma, iv_r=dma,
+        ch_s=dma((2,)), ch_r=dma((nblk, bm // pr)), la_s=dma, la_r=dma((nblk,)),
         p_s=dma, p_r=dma((nu,)), pf_r=dma((nu,)), h_s=dma, hn_r=dma((nu,)), hb_r=dma((nblk,)),
         lr_s=dma, lr_r=dma((nblk,)), g_s=dma, g_r=dma((nblk,)),
         t_s=dma, t_r=dma, pp_s=dma, pp_r=dma, pb_s=dma, pb_r=dma, c_s=dma, c_r=dma, o_s=dma, o_r=dma,
         tq_s=dma, tq_r=dma, tc_s=dma, tc_r=dma,
     )
-    dims = (nq, nc, r, nblk, bm, nh, hw, min(3, nu - 1), w * nc)
+    dims = (nq, nc, r, nblk, bm, pr, nh, hw, w * nc)
     vspec, aspec = pl.BlockSpec(memory_space=pltpu.VMEM), pl.BlockSpec(memory_space=pl.ANY)
     return pl.pallas_call(
         functools.partial(fast_kernel, dims, tuple(scratch)),

time: 101 us -> 95.3 us (0.944)
  Pallas kernels: 99.4 us -> 93.8 us
    pallas_call x1, Pallas kernels: 99.4 us -> 93.8 us  [per_device_fast(): pl.pallas_call(functools.partial(fast_kernel, dims, tuple(scratch)), out_...]
where the time goes in v3:
time: 95.3 us; the launch traced here: 95.1 us
  Pallas kernels  93.8 us (98%)
  local copies, waits for them, and re-layouts  1.3 us (1%)
    pallas_call x1, Pallas kernels, per_device_fast(): pl.pallas_call(functools.partial(fast_kernel, dims, tuple(scratch)), out_...  93.8 us

profile of v3, /device:TPU:0, one launch (start us, length us, event | category | flops | bytes accessed | tf_op | source)
XLA Modules:
  0.0 95.1 jit_solution(2298926668956793642)
XLA Ops:
  0.0 93.8 %shard_map.73 = f32[16,100]{1,0:T(8,128)} custom-call(bf16[128,512]{1,0:T(8,128)(2,1)} %hid.1, s32[4]{0:T(128)} %lens.1, bf16[1024,1792]{1,0:T(8,128)(2,1)} %gate_h.1, bf16[1024,1792]{1,0:T(8,128)(2,1)} %up_h.1, bf16[1792,1024]{1,0:T(8,128)(2,1)} %down_h.1, bf16[512,1024]{1,0:T(8,128)(2,1)} %code_h.1, bf16[512,1024]{1,0:T(8,128)(2,1)} %corp_h.1), custom_call_target="tpu_custom_call" | custom-call | tf_op jit(solution)/shard_map/pallas_call | solution.py:948
  93.8 1.3 %copy.9 = f32[16,100]{1,0:T(8,128)} copy(f32[16,100]{1,0:T(8,128)} %shard_map.73) | data formatting | bytes 12800

commit v4 on v3

--- a/solution.py
+++ b/solution.py
@@ -510,7 +510,7 @@
 
 
 def fast_kernel(dims, names, hid, lens, gate_h, up_h, down_h, code_h, corp_h, out, *refs):
-    nq, nc, r, nblk, bm, pr, nh, hw, d_all = dims
+    nq, nc, r, nblk, bm, nh, hw, d_all = dims
     s = types.SimpleNamespace(**dict(zip(names, refs)))
     q = lax.axis_index("query")
     c = lax.axis_index("corpus")
@@ -526,8 +526,9 @@
     bw = s.codew.shape[2] // nq
     gate, up, code, corp = s.gu.at[0], s.gu.at[1], s.codew.at[0], s.codew.at[1]
 
-    first = pltpu.make_async_copy(hid, s.colbuf.at[q], s.w_s.at[0])
-    first.start()
+    fq = w // nq
+    for i in range(nq):
+        pltpu.make_async_copy(hid.at[:, pl.ds(i * fq, fq)], s.hidq.at[i], s.w_s.at[0]).start()
     counts = pltpu.make_async_copy(lens, s.lens_s, s.w_s.at[1])
     counts.start()
     for a, b, k in ((gate_h, gate, 2), (up_h, up, 2), (down_h, s.down, 3), (code_h, code, 4), (corp_h, corp, 4)):
@@ -565,9 +566,11 @@
     for k in range(1, nc):
         pl.semaphore_signal(barrier, inc=1, device_id=(q, rc(k)), device_id_type=pl.DeviceIdType.MESH)
 
-    first.wait()
-    squares = jnp.square(s.colbuf[q].astype(F32))
-    s.st_send[...] = lax.dot_general(jnp.ones((8, w), F32), squares, (((1,), (1,)), ((), ())),
+    loaded(s.hidq, 0)
+    squares = jnp.square(s.hidq[0].astype(F32))
+    for i in range(1, nq):
+        squares = squares + jnp.square(s.hidq[i].astype(F32))
+    s.st_send[...] = lax.dot_general(jnp.ones((8, fq), F32), squares, (((1,), (1,)), ((), ())),
                                      precision=lax.Precision.HIGHEST, preferred_element_type=F32)
     counts.wait()
     slot_query = lax.broadcasted_iota(jnp.int32, (8, slots), 1) // SEQ
@@ -581,18 +584,10 @@
     side_a = q + 1 - 2 * lax.rem(q, 2)
     side_b = q + 2 - 4 * (q // 2)
     far = nq - 1 - q
-    opposite = nq - 1 - g
-    helper = g + 1 - 2 * lax.rem(g, 2)
-    upper, lower = pl.ds(0, slots // 2), pl.ds(slots // 2, slots // 2)
-
-    @pl.when(jnp.logical_and(q != g, q != opposite))
-    def _():
-        rcopy(s.colbuf.at[q], s.colbuf.at[q], s.a_s, s.a_r, (g, c)).start()
-
-    @pl.when(q == opposite)
-    def _():
-        rcopy(s.colbuf.at[q, lower], s.colbuf.at[q, lower], s.a_s, s.ah_r, (helper, c)).start()
-        rcopy(s.colbuf.at[q, upper], s.colbuf.at[q, upper], s.a_s, s.a_r, (g, c)).start()
+
+    for k in range(1, nq):
+        rcopy(s.hidq.at[rq(k)], s.colbuf.at[q], s.a_s, s.a_r, (rq(k), c)).start()
+    s.colbuf[q] = s.hidq[q]
 
     to_query(s.lens_all.at[q], s.lens_all, s.l_s, s.l_r)
     to_corpus(s.st_send, s.st_recv, s.st_s, s.st_r)
@@ -605,11 +600,6 @@
     pos = mm(valid.astype(F32).astype(BF16), before.astype(F32).astype(BF16)).astype(jnp.int32)
     pos = jnp.where(valid, pos, -1)[:1]
 
-    @pl.when(q == helper)
-    def _():
-        got(s.colbuf.at[0, lower], s.ah_r)
-        rcopy(s.colbuf.at[opposite, lower], s.colbuf.at[opposite, lower], s.ah_s, s.a_r, (g, c)).start()
-
     got(s.st_recv.at[pl.ds(0, nc - 1)], s.st_r)
     stat = s.st_recv[0]
     for i in range(1, nc):
@@ -617,43 +607,29 @@
     s.inv_all[q] = lax.rsqrt(stat / d_all + epsilon)
     to_query(s.inv_all.at[q], s.inv_all, s.iv_s, s.iv_r)
 
-    def piece(b, p):
-        return s.xall.at[j, b, pl.ds(p * pr, pr)]
-
-    def down_chain(b, p):
-        return rcopy(piece(b, p), piece(b, p), s.ch_s.at[0], s.ch_r.at[b, p], (q, jnp.maximum(c - r, 0)))
-
-    def up_chain(b, p):
-        return rcopy(piece(b, p), piece(b, p), s.ch_s.at[1], s.ch_r.at[b, p], (q, jnp.minimum(c + r, nc - 1)))
-
-    def side(b, p, k):
-        return rcopy(piece(b, p), piece(b, p), s.la_s, s.la_r.at[b], (q, g * r + lane(k)))
-
-    sends_up = jnp.logical_and(g >= q, g < ng - 1)
-    sends_down = jnp.logical_and(g <= q, g > 0)
-
-    def pass_on(b, p):
-        @pl.when(sends_up)
-        def _():
-            up_chain(b, p).start()
-
-        @pl.when(sends_down)
-        def _():
-            down_chain(b, p).start()
-
-        for k in range(1, r):
-            side(b, p, k).start()
-
-    @pl.when(q == g)
-    def _():
-        got(s.colbuf.at[pl.ds(0, nq - 1)], s.a_r)
-        stacked = s.colbuf[...].reshape(total, w)
-        for b in range(nblk):
-            row = lax.broadcasted_iota(jnp.int32, (bm, total), 0) + b * bm
-            pick = (pos == row).astype(F32).astype(BF16)
-            s.xall[j, b] = mm(pick, stacked).astype(BF16)
-            for p in range(bm // pr):
-                pass_on(b, p)
+    def side(b, k):
+        return rcopy(s.xall.at[j, b], s.xall.at[j, b], s.la_s, s.la_r.at[b], (q, g * r + lane(k)))
+
+    def spread(b, k):
+        t = lax.rem(g + k, ng)
+        return rcopy(s.xpk.at[b], s.xall.at[j, b, q], s.x_s, s.x_r.at[b], (g, t * r + j))
+
+    got(s.colbuf.at[pl.ds(0, nq - 1)], s.a_r)
+    stacked = s.colbuf[...].reshape(total, fq)
+    for b in range(nblk):
+        row = lax.broadcasted_iota(jnp.int32, (bm, total), 0) + b * bm
+        pick = (pos == row).astype(F32).astype(BF16)
+        s.xpk[b] = mm(pick, stacked).astype(BF16)
+        for k in range(ng - 1, 0, -1):
+            spread(b, k).start()
+
+        @pl.when(q != g)
+        def _(b=b):
+            spread(b, 0).start()
+
+        @pl.when(q == g)
+        def _(b=b):
+            s.xall[j, b, q] = s.xpk[b]
 
     got(s.inv_all.at[pl.ds(0, nq - 1)], s.iv_r)
     inv_row = jnp.concatenate([s.inv_all[i] for i in range(nq)], axis=1)[:1]
@@ -687,17 +663,25 @@
         one, two = sides(n)
         return rcopy(s.hall.at[n, one], s.hall.at[n, one], s.h_s, sem, (two, c))
 
-    def products(b):
+    def fetch(b):
         @pl.when(q != g)
         def _():
-            for p in range(bm // pr):
-                up_chain(b, p).wait_recv()
-                pass_on(b, p)
-
+            got(s.xall.at[0, b], s.x_r.at[b])
+
+        @pl.when(q == g)
+        def _():
+            got(s.xall.at[0, b, pl.ds(0, nq - 1)], s.x_r.at[b])
+
+        for k in range(1, r):
+            side(b, k).start()
+
+    def products(b):
         got(s.xall.at[pl.ds(0, r - 1), b], s.la_r.at[b])
         scale = s.inv_c[b][:, :1]
         for i in range(r):
-            s.xn[:, i * w:(i + 1) * w] = (s.xall[i, b].astype(F32) * scale).astype(BF16)
+            for k in range(nq):
+                at = i * w + k * fq
+                s.xn[:, at:at + fq] = (s.xall[i, b, k].astype(F32) * scale).astype(BF16)
         xb = s.xn[...]
         for h in range(nh):
             n = b * nh + h
@@ -763,9 +747,15 @@
         for h in range(nh):
             unit(b * nh + h)
 
-    stages = (products, functools.partial(units, pass_unit), functools.partial(units, reduce_unit),
+    def fetch_next(b):
+        @pl.when(b + 1 < nblk)
+        def _():
+            fetch(b + 1)
+
+    fetch(0)
+    stages = (products, fetch_next, functools.partial(units, pass_unit), functools.partial(units, reduce_unit),
               functools.partial(units, relay_unit), down_block, sum_block)
-    delays = (0,1,3,4,6,7)
+    delays = (0,0,1,2,3,4,5)
 
     def turn(t, carry):
         for stage, delay in zip(stages, delays):
@@ -780,7 +770,9 @@
     row = (row // pm) * bm + (j * ng + g) * pm + lax.rem(row, pm)
     own_rows = (lax.broadcasted_iota(jnp.int32, (nblk * pm, nreal), 1) == row).astype(F32).astype(BF16)
     for i in range(r):
-        s.res[:, i * w:(i + 1) * w] = mm(own_rows, s.xall[i].reshape(nreal, w))
+        for k in range(nq):
+            at = i * w + k * fq
+            s.res[:, at:at + fq] = mm(own_rows, s.xall[i, :, k].reshape(nreal, fq))
 
     for b in range(nblk):
         total_b = s.gsend[b, g].astype(F32)
@@ -831,13 +823,13 @@
     def _():
         got(s.pblk.at[0], s.pb_r)
 
-    s.cpart[...] = mm(s.pblk[0], code[:, pl.ds(pl.multiple_of(q * bw, bw), bw)]).astype(BF16)
+    s.cpart[...] = mm(s.pblk[0], code[:, pl.ds(pl.multiple_of(q * bw, bw), bw)])
     to_corpus(s.cpart, s.crecv, s.c_s, s.c_r)
     s.crecv[c] = s.cpart[...]
     got(s.crecv.at[pl.ds(0, nc - 1)], s.c_r)
-    csum = s.crecv[0].astype(F32)
+    csum = s.crecv[0]
     for i in range(1, nc):
-        csum = csum + s.crecv[i].astype(F32)
+        csum = csum + s.crecv[i]
     s.codes[q] = csum.astype(BF16)
     to_query(s.codes.at[q], s.codes, s.o_s, s.o_r)
     got(s.codes.at[pl.ds(0, nq - 1)], s.o_r)
@@ -862,21 +854,15 @@
     sent(s.st_recv.at[pl.ds(0, nc - 1)], s.st_s)
     sent(s.inv_all.at[pl.ds(0, nq - 1)], s.iv_s)
 
+    sent(s.colbuf.at[pl.ds(0, nq - 1)], s.a_s)
+
     @pl.when(q != g)
     def _():
-        sent(s.colbuf.at[0], s.a_s)
-
-    @pl.when(q == helper)
-    def _():
-        sent(s.colbuf.at[0, lower], s.ah_s)
-
-    @pl.when(sends_down)
-    def _():
-        sent(s.xall.at[0], s.ch_s.at[0])
-
-    @pl.when(sends_up)
-    def _():
-        sent(s.xall.at[0], s.ch_s.at[1])
+        sent(s.xall.at[0], s.x_s)
+
+    @pl.when(q == g)
+    def _():
+        sent(s.xall.at[0, :, pl.ds(0, nq - 1)], s.x_s)
 
     sent(s.xall.at[pl.ds(0, r - 1)], s.la_s)
     sent(s.psend.at[:, pl.ds(0, 3)], s.p_s)
@@ -912,7 +898,6 @@
     dq, ffc = gate_weight.shape
     bm = 8 * nc
     nblk = nreal // bm
-    pr = PIECE if bm % PIECE == 0 else bm
     nh = halves_of(ffc)
     hw = ffc // nh
     nu = nblk * nh
@@ -925,7 +910,7 @@
     scratch = dict(
         gu=vm((2,) + gate_weight.shape, BF16), down=vm(down_weight.shape, BF16), codew=vm((2,) + code_weight.shape, BF16),
         lens_s=pltpu.SMEM(lengths.shape, jnp.int32),
-        colbuf=vm((nq, slots, w), BF16), lens_all=vm((nq, 8, slots), jnp.int32), xall=vm((r, nblk, bm, w), BF16),
+        hidq=vm((nq, slots, w // nq), BF16), colbuf=vm((nq, slots, w // nq), BF16), xpk=vm((nblk, bm, w // nq), BF16), lens_all=vm((nq, 8, slots), jnp.int32), xall=vm((r, nblk, nq, bm, w // nq), BF16),
         xn=vm((bm, dq), BF16), inv_c=vm((nblk, bm, LANES), F32),
         st_send=vm((8, slots), F32), st_recv=vm((nc, 8, slots), F32), inv_all=vm((nq, 8, slots), F32),
         psend=vm((nu, nq, 2, qm, hw), BF16), precv=vm((nu, 4, 2, qm, hw), BF16), pown=vm((nu, 2, qm, hw), F32), full=vm((nh, 2, bm, hw), F32),
@@ -934,16 +919,16 @@
         gsend=vm((nblk, ng, pm, dq), BF16), grecv=vm((nblk, ng, pm, dq), BF16), res=vm((tb, dq), F32),
         t_send=vm((tb, LANES), F32), t_recv=vm((nq, tb, LANES), F32),
         pp=vm((r, nqueries, w), BF16), prc=vm((nc, nqueries, w), BF16), pblk=vm((nq, nqueries, w), BF16),
-        cpart=vm((nqueries, bw), BF16), crecv=vm((nc, nqueries, bw), BF16), codes=vm((nq, nqueries, bw), BF16),
+        cpart=vm((nqueries, bw), F32), crecv=vm((nc, nqueries, bw), F32), codes=vm((nq, nqueries, bw), BF16),
         top_q=vm((nq, nqueries, LANES), F32), top_c=vm((nc, nqueries, LANES), F32),
-        w_s=dma((5,)), l_s=dma, l_r=dma, a_s=dma, a_r=dma, ah_s=dma, ah_r=dma, st_s=dma, st_r=dma, iv_s=dma, iv_r=dma,
-        ch_s=dma((2,)), ch_r=dma((nblk, bm // pr)), la_s=dma, la_r=dma((nblk,)),
+        w_s=dma((5,)), l_s=dma, l_r=dma, a_s=dma, a_r=dma, st_s=dma, st_r=dma, iv_s=dma, iv_r=dma,
+        x_s=dma, x_r=dma((nblk,)), la_s=dma, la_r=dma((nblk,)),
         p_s=dma, p_r=dma((nu,)), pf_r=dma((nu,)), h_s=dma, hn_r=dma((nu,)), hb_r=dma((nblk,)),
         lr_s=dma, lr_r=dma((nblk,)), g_s=dma, g_r=dma((nblk,)),
         t_s=dma, t_r=dma, pp_s=dma, pp_r=dma, pb_s=dma, pb_r=dma, c_s=dma, c_r=dma, o_s=dma, o_r=dma,
         tq_s=dma, tq_r=dma, tc_s=dma, tc_r=dma,
     )
-    dims = (nq, nc, r, nblk, bm, pr, nh, hw, w * nc)
+    dims = (nq, nc, r, nblk, bm, nh, hw, w * nc)
     vspec, aspec = pl.BlockSpec(memory_space=pltpu.VMEM), pl.BlockSpec(memory_space=pl.ANY)
     return pl.pallas_call(
         functools.partial(fast_kernel, dims, tuple(scratch)),
@@ -959,7 +944,7 @@
 def per_device(nq, nc, hidden_in, *rest):
     slots, w = hidden_in.shape
     nreal = nq * slots * REAL_NUM // REAL_DEN
-    fits = nreal % (8 * nc) == 0 and w % LANES == 0 and rest[4].shape == rest[5].shape
+    fits = nreal % (8 * nc) == 0 and w % (nq * LANES) == 0 and rest[4].shape == rest[5].shape
     body = per_device_fast if fits else per_device_general
     return body(nq, nc, hidden_in, *rest)
 

time: 95.3 us -> 88.3 us (0.927)
  Pallas kernels: 93.8 us -> 86.8 us
    pallas_call x1, Pallas kernels: 93.8 us -> 86.8 us  [per_device_fast(): pl.pallas_call(functools.partial(fast_kernel, dims, tuple(scratch)), out_...]
where the time goes in v4:
time: 88.3 us; the launch traced here: 88.1 us
  Pallas kernels  86.8 us (98%)
  local copies, waits for them, and re-layouts  1.3 us (1%)
    pallas_call x1, Pallas kernels, per_device_fast(): pl.pallas_call(functools.partial(fast_kernel, dims, tuple(scratch)), out_...  86.8 us

profile of v4, /device:TPU:0, one launch (start us, length us, event | category | flops | bytes accessed | tf_op | source)
XLA Modules:
  0.0 88.1 jit_solution(8067569957618554114)
XLA Ops:
  0.0 86.8 %shard_map.73 = f32[16,100]{1,0:T(8,128)} custom-call(bf16[128,512]{1,0:T(8,128)(2,1)} %hid.1, s32[4]{0:T(128)} %lens.1, bf16[1024,1792]{1,0:T(8,128)(2,1)} %gate_h.1, bf16[1024,1792]{1,0:T(8,128)(2,1)} %up_h.1, bf16[1792,1024]{1,0:T(8,128)(2,1)} %down_h.1, bf16[512,1024]{1,0:T(8,128)(2,1)} %code_h.1, bf16[512,1024]{1,0:T(8,128)(2,1)} %corp_h.1), custom_call_target="tpu_custom_call" | custom-call | tf_op jit(solution)/shard_map/pallas_call | solution.py:933
  86.8 1.3 %copy.9 = f32[16,100]{1,0:T(8,128)} copy(f32[16,100]{1,0:T(8,128)} %shard_map.73) | data formatting | bytes 12800

commit v5 on v4

--- a/solution.py
+++ b/solution.py
@@ -509,6 +509,89 @@
     )(hidden_in, lens, gate_weight, up_weight, down_weight, code_weight, corpus_codes)
 
 
+def compare(v, size, step, flip, inner):
+    part = len(v)
+    sub = lax.broadcasted_iota(jnp.int32, v[0].shape, 0)
+    across = step < part if inner else step >= 8
+    if size >= LANES:
+        up = [0] * part
+    elif size < part:
+        up = [int((i & size) != 0) for i in range(part)]
+    else:
+        up = [((sub & (size // part)) != 0).astype(jnp.int32)] * part
+    masks = {}
+
+    def high(i, low, name):
+        key = (name, up[i] if isinstance(up[i], int) else -1)
+        if key not in masks:
+            masks[key] = (flip ^ up[i] ^ low) == 0
+        return masks[key]
+
+    v = list(v)
+    if across:
+        hop = step if inner else step // 8
+        for i in range(part):
+            if i & hop == 0:
+                a, b = v[i], v[i | hop]
+                most, least = jnp.maximum(a, b), jnp.minimum(a, b)
+                pick = high(i, 0, 0)
+                v[i], v[i | hop] = jnp.where(pick, most, least), jnp.where(pick, least, most)
+        return v
+    s = step // part if inner else step
+    bit = (sub & s) != 0
+    low = bit.astype(jnp.int32)
+    for i in range(part):
+        x = v[i]
+        other = pltpu.roll(x, 4, 0) if s == 4 else jnp.where(bit, pltpu.roll(x, s, 0), pltpu.roll(x, 8 - s, 0))
+        v[i] = jnp.where(high(i, low, 1), jnp.maximum(x, other), jnp.minimum(x, other))
+    return v
+
+
+def columns(lists):
+    cols = jnp.concatenate([lists] * (LANES // lists.shape[0]), axis=0).T
+    return [cols[i:i + 8] for i in range(0, LANES, 8)]
+
+
+def merge_columns(v, count, rows, lone, inner):
+    lane = lax.broadcasted_iota(jnp.int32, v[0].shape, 1)
+    half = count // 2
+    while half >= rows:
+        v = [jnp.maximum(x, pltpu.roll(x, LANES - half, 1)) for x in v]
+        if half > rows:
+            flip = (lax.rem(lane, half) >= half // 2).astype(jnp.int32)
+        else:
+            flip = jnp.zeros_like(lane) + jnp.asarray(lone, jnp.int32)
+        step = LANES // 2
+        while step:
+            v = compare(v, LANES, step, flip, inner)
+            step //= 2
+        half //= 2
+    return v
+
+
+def top_rows(lists, rows, lone, board):
+    count = lists.shape[0]
+    v = columns(lists)
+    lane = lax.broadcasted_iota(jnp.int32, v[0].shape, 1)
+    flip = (lax.rem(lane, count) >= count // 2).astype(jnp.int32)
+    size = 2
+    while size <= LANES:
+        step = size // 2
+        while step:
+            v = compare(v, size, step, flip, True)
+            step //= 2
+        size *= 2
+    v = merge_columns(v, count, rows, lone, True)
+    for i, x in enumerate(v):
+        board[pl.ds(i, 8, stride=len(v)), :] = x
+    return board[...].T[:rows]
+
+
+def merge_rows(lists, rows, lone):
+    v = merge_columns(columns(lists), lists.shape[0], rows, lone, False)
+    return jnp.concatenate(v, axis=0).T[:rows]
+
+
 def fast_kernel(dims, names, hid, lens, gate_h, up_h, down_h, code_h, corp_h, out, *refs):
     nq, nc, r, nblk, bm, nh, hw, d_all = dims
     s = types.SimpleNamespace(**dict(zip(names, refs)))
@@ -755,7 +838,7 @@
     fetch(0)
     stages = (products, fetch_next, functools.partial(units, pass_unit), functools.partial(units, reduce_unit),
               functools.partial(units, relay_unit), down_block, sum_block)
-    delays = (0,0,1,2,3,4,5)
+    delays = (0, 0, 1, 2, 3, 4, 5)
 
     def turn(t, carry):
         for stage, delay in zip(stages, delays):
@@ -839,15 +922,15 @@
 
     blocks = corp.shape[0] // LANES
     lists = jnp.concatenate([scores[:, i * LANES:(i + 1) * LANES] for i in range(blocks)], axis=0)
-    best = merge_all(sort_lanes(lists), nqueries, q >= nq // 2)
+    best = top_rows(lists, nqueries, q >= nq // 2, s.board)
     s.top_q[q] = best
     to_query(s.top_q.at[q], s.top_q, s.tq_s, s.tq_r)
     got(s.top_q.at[pl.ds(0, nq - 1)], s.tq_r)
-    best = merge_all(s.top_q[...].reshape(nq * nqueries, LANES), nqueries, c >= nc // 2)
+    best = merge_rows(s.top_q[...].reshape(nq * nqueries, LANES), nqueries, c >= nc // 2)
     s.top_c[c] = best
     to_corpus(s.top_c.at[c], s.top_c, s.tc_s, s.tc_r)
     got(s.top_c.at[pl.ds(0, nc - 1)], s.tc_r)
-    best = merge_all(s.top_c[...].reshape(nc * nqueries, LANES), nqueries, False)
+    best = merge_rows(s.top_c[...].reshape(nc * nqueries, LANES), nqueries, False)
     out[...] = best[:, :TOPK]
 
     sent(s.lens_all.at[pl.ds(0, nq - 1)], s.l_s)
@@ -920,7 +1003,7 @@
         t_send=vm((tb, LANES), F32), t_recv=vm((nq, tb, LANES), F32),
         pp=vm((r, nqueries, w), BF16), prc=vm((nc, nqueries, w), BF16), pblk=vm((nq, nqueries, w), BF16),
         cpart=vm((nqueries, bw), F32), crecv=vm((nc, nqueries, bw), F32), codes=vm((nq, nqueries, bw), BF16),
-        top_q=vm((nq, nqueries, LANES), F32), top_c=vm((nc, nqueries, LANES), F32),
+        top_q=vm((nq, nqueries, LANES), F32), top_c=vm((nc, nqueries, LANES), F32), board=vm((LANES, LANES), F32),
         w_s=dma((5,)), l_s=dma, l_r=dma, a_s=dma, a_r=dma, st_s=dma, st_r=dma, iv_s=dma, iv_r=dma,
         x_s=dma, x_r=dma((nblk,)), la_s=dma, la_r=dma((nblk,)),
         p_s=dma, p_r=dma((nu,)), pf_r=dma((nu,)), h_s=dma, hn_r=dma((nu,)), hb_r=dma((nblk,)),
@@ -944,7 +1027,9 @@
 def per_device(nq, nc, hidden_in, *rest):
     slots, w = hidden_in.shape
     nreal = nq * slots * REAL_NUM // REAL_DEN
-    fits = nreal % (8 * nc) == 0 and w % (nq * LANES) == 0 and rest[4].shape == rest[5].shape
+    nqueries = nq * rest[0].shape[0]
+    lists = nqueries * max(nc, nq, rest[5].shape[0] // LANES)
+    fits = lists <= LANES and LANES % lists == 0 and nreal % (8 * nc) == 0 and w % (nq * LANES) == 0 and rest[4].shape == rest[5].shape
     body = per_device_fast if fits else per_device_general
     return body(nq, nc, hidden_in, *rest)
 

time: 88.3 us -> 84.1 us (0.952)
  Pallas kernels: 86.8 us -> 82.6 us
    pallas_call x1, Pallas kernels: 86.8 us -> 82.6 us  [per_device_fast(): pl.pallas_call(functools.partial(fast_kernel, dims, tuple(scratch)), out_...]
where the time goes in v5:
time: 84.1 us; the launch traced here: 83.9 us
  Pallas kernels  82.6 us (98%)
  local copies, waits for them, and re-layouts  1.3 us (2%)
    pallas_call x1, Pallas kernels, per_device_fast(): pl.pallas_call(functools.partial(fast_kernel, dims, tuple(scratch)), out_...  82.6 us

profile of v5, /device:TPU:0, one launch (start us, length us, event | category | flops | bytes accessed | tf_op | source)
XLA Modules:
  0.0 83.9 jit_solution(444362231094269560)
XLA Ops:
  0.0 82.6 %shard_map.73 = f32[16,100]{1,0:T(8,128)} custom-call(bf16[128,512]{1,0:T(8,128)(2,1)} %hid.1, s32[4]{0:T(128)} %lens.1, bf16[1024,1792]{1,0:T(8,128)(2,1)} %gate_h.1, bf16[1024,1792]{1,0:T(8,128)(2,1)} %up_h.1, bf16[1792,1024]{1,0:T(8,128)(2,1)} %down_h.1, bf16[512,1024]{1,0:T(8,128)(2,1)} %code_h.1, bf16[512,1024]{1,0:T(8,128)(2,1)} %corp_h.1), custom_call_target="tpu_custom_call" | custom-call | tf_op jit(solution)/shard_map/pallas_call | solution.py:1016
  82.6 1.3 %copy.9 = f32[16,100]{1,0:T(8,128)} copy(f32[16,100]{1,0:T(8,128)} %shard_map.73) | data formatting | bytes 12800

commit v6 on v5

--- a/solution.py
+++ b/solution.py
@@ -604,17 +604,17 @@
     total = nq * slots
     nqueries = total // SEQ
     nreal = nblk * bm
-    qm, lm, pm = bm // nq, bm // r, bm // nc
+    qm, gm = bm // nq, bm // ng
     nu = nblk * nh
-    bw = s.codew.shape[2] // nq
-    gate, up, code, corp = s.gu.at[0], s.gu.at[1], s.codew.at[0], s.codew.at[1]
+    bw = s.codeq.shape[1]
+    gate, up, corp = s.gu.at[0], s.gu.at[1], s.corp
 
     fq = w // nq
     for i in range(nq):
         pltpu.make_async_copy(hid.at[:, pl.ds(i * fq, fq)], s.hidq.at[i], s.w_s.at[0]).start()
     counts = pltpu.make_async_copy(lens, s.lens_s, s.w_s.at[1])
     counts.start()
-    for a, b, k in ((gate_h, gate, 2), (up_h, up, 2), (down_h, s.down, 3), (code_h, code, 4), (corp_h, corp, 4)):
+    for a, b, k in ((gate_h, gate, 2), (up_h, up, 2), (down_h, s.down, 3), (code_h.at[:, pl.ds(pl.multiple_of(q * bw, bw), bw)], s.codeq, 4), (corp_h, corp, 5)):
         pltpu.make_async_copy(a, b, s.w_s.at[k]).start()
 
     def loaded(ref, k):
@@ -643,7 +643,11 @@
         for k in range(1, nc):
             rcopy(src, ref.at[c], ss, rs, (q, rc(k))).start()
 
+    others = [(n, k) for n in range(nq) for k in range(r) if n or k]
     barrier = pltpu.get_barrier_semaphore()
+    for n, k in others:
+        if n and k:
+            pl.semaphore_signal(barrier, inc=1, device_id=(rq(n), g * r + lane(k)), device_id_type=pl.DeviceIdType.MESH)
     for k in range(1, nq):
         pl.semaphore_signal(barrier, inc=1, device_id=(rq(k), c), device_id_type=pl.DeviceIdType.MESH)
     for k in range(1, nc):
@@ -662,7 +666,7 @@
         own_lens = jnp.where(slot_query == k, s.lens_s[k], own_lens)
     s.lens_all[q] = own_lens
 
-    pl.semaphore_wait(barrier, nq - 1 + nc - 1)
+    pl.semaphore_wait(barrier, nq - 1 + nc - 1 + (nq - 1) * (r - 1))
 
     side_a = q + 1 - 2 * lax.rem(q, 2)
     side_b = q + 2 - 4 * (q // 2)
@@ -811,18 +815,20 @@
             n = b * nh + h
             term = mm(s.hall[n].reshape(bm, hw), s.down[h * hw:(h + 1) * hw, :])
             part = term if part is None else part + term
+        s.acc[b] = part
         for t in range(r):
-            s.lsend[b, t] = part[t * lm:(t + 1) * lm].astype(BF16)
+            s.lsend[b, t] = part[:, t * w:(t + 1) * w].astype(BF16)
         for k in range(1, r):
             lane_send(b, k).start()
 
     def sum_block(b):
-        mine = s.lsend[b, j].astype(F32)
+        mine = s.acc[b, :, pl.ds(pl.multiple_of(j * w, w), w)]
         got(s.lrecv.at[b, pl.ds(0, r - 1)], s.lr_r.at[b])
         for k in range(1, r):
             mine = mine + s.lrecv[b, lane(k)].astype(F32)
+        s.mine[b] = mine
         for t in range(ng):
-            s.gsend[b, t] = mine[t * pm:(t + 1) * pm].astype(BF16)
+            s.gsend[b, t] = mine[t * gm:(t + 1) * gm].astype(BF16)
         for k in range(1, ng):
             group_send(b, k).start()
 
@@ -849,25 +855,24 @@
 
     loaded(s.down, 3)
     lax.fori_loop(0, nblk + delays[-1], turn, 0)
-    row = lax.broadcasted_iota(jnp.int32, (nblk * pm, nreal), 0)
-    row = (row // pm) * bm + (j * ng + g) * pm + lax.rem(row, pm)
-    own_rows = (lax.broadcasted_iota(jnp.int32, (nblk * pm, nreal), 1) == row).astype(F32).astype(BF16)
-    for i in range(r):
+    own = pl.ds(pl.multiple_of(g * gm, gm), gm)
+    for b in range(nblk):
         for k in range(nq):
-            at = i * w + k * fq
-            s.res[:, at:at + fq] = mm(own_rows, s.xall[i, :, k].reshape(nreal, fq))
-
+            s.res[b * gm:(b + 1) * gm, k * fq:(k + 1) * fq] = s.xall[j, b, k, own].astype(F32)
     for b in range(nblk):
-        total_b = s.gsend[b, g].astype(F32)
+        total_b = s.mine[b, own]
         got(s.grecv.at[b, pl.ds(0, ng - 1)], s.g_r.at[b])
         for k in range(1, ng):
             total_b = total_b + s.grecv[b, lax.rem(g + k, ng)].astype(F32)
-        s.res[b * pm:(b + 1) * pm, :] = s.res[b * pm:(b + 1) * pm, :] + total_b
+        s.res[b * gm:(b + 1) * gm] = s.res[b * gm:(b + 1) * gm] + total_b
     residual = s.res[...]
-    tb = nblk * pm
-
-    s.t_send[...] = jnp.broadcast_to(jnp.sum(residual * residual, axis=1, keepdims=True), (tb, LANES))
-    to_query(s.t_send, s.t_recv, s.t_s, s.t_r)
+    tb = nblk * gm
+
+    sums = lax.dot_general(jnp.ones((8, w), F32), residual * residual, (((1,), (1,)), ((), ())),
+                           precision=lax.Precision.HIGHEST, preferred_element_type=F32)
+    s.t_send[...] = jnp.concatenate([sums, jnp.zeros((8, LANES - tb), F32)], axis=1)
+    for n, k in others:
+        rcopy(s.t_send, s.t_recv.at[q * r + j], s.t_s, s.t_r, (rq(n), g * r + lane(k))).start()
     qrow = lax.broadcasted_iota(jnp.int32, (nqueries, total), 0)
     qslot = lax.broadcasted_iota(jnp.int32, (nqueries, total), 1)
     lens_b = jnp.broadcast_to(lens_row[:1], (nqueries, total)).astype(F32)
@@ -875,38 +880,38 @@
     len_col = jnp.sum(jnp.where(qslot == qrow * SEQ, lens_b, 0.0), axis=1, keepdims=True)
     off_col = jnp.sum(jnp.where(qslot < qrow * SEQ, vals_b, 0.0), axis=1, keepdims=True)
     prow = lax.broadcasted_iota(jnp.int32, (nqueries, tb), 1)
-    prow = ((prow // pm) * bm + (j * ng + g) * pm + lax.rem(prow, pm)).astype(F32)
+    prow = ((prow // gm) * bm + g * gm + lax.rem(prow, gm)).astype(F32)
     member = jnp.where(jnp.logical_and(prow >= off_col, prow < off_col + len_col), 1.0, 0.0)
     tsum = s.t_send[...]
-    got(s.t_recv.at[pl.ds(0, nq - 1)], s.t_r)
-    for k in range(1, nq):
-        tsum = tsum + s.t_recv[rq(k)]
-    final = residual * lax.rsqrt(tsum[:, :1] / d_all + epsilon)
-    pooled_part = mm(member, final, lax.Precision.HIGHEST)
-    for i in range(r):
-        s.pp[i] = pooled_part[:, i * w:(i + 1) * w].astype(BF16)
-    for i in range(r):
-        @pl.when(c != q * r + i)
-        def _(i=i):
-            rcopy(s.pp.at[i], s.prc.at[c], s.pp_s, s.pp_r, (q, q * r + i)).start()
+    got(s.t_recv.at[pl.ds(0, len(others))], s.t_r)
+    for n, k in others:
+        tsum = tsum + s.t_recv[rq(n) * r + lane(k)]
+    inv_own = lax.rsqrt(tsum[:1, :tb] / d_all + epsilon)
+    pooled_part = mm(member * inv_own, residual, lax.Precision.HIGHEST)
+    s.pp[...] = pooled_part
+
+    @pl.when(g != q)
+    def _():
+        rcopy(s.pp, s.prc.at[g], s.pp_s, s.pp_r, (q, q * r + j)).start()
 
     @pl.when(g == q)
     def _():
-        pooled = s.pp[j].astype(F32)
-        got(s.prc.at[pl.ds(0, nc - 1)], s.pp_r)
-        for k in range(1, nc):
-            pooled = pooled + s.prc[rc(k)].astype(F32)
+        pooled = pooled_part
+        got(s.prc.at[pl.ds(0, ng - 1)], s.pp_r)
+        for k in range(1, ng):
+            pooled = pooled + s.prc[lax.rem(g + k, ng)]
         s.pblk[0] = (pooled / len_col).astype(BF16)
         for k in range(1, nq):
             rcopy(s.pblk.at[0], s.pblk.at[0], s.pb_s, s.pb_r, (rq(k), c)).start()
 
-    loaded(s.codew, 4)
+    loaded(s.codeq, 4)
+    loaded(s.corp, 5)
 
     @pl.when(g != q)
     def _():
         got(s.pblk.at[0], s.pb_r)
 
-    s.cpart[...] = mm(s.pblk[0], code[:, pl.ds(pl.multiple_of(q * bw, bw), bw)])
+    s.cpart[...] = mm(s.pblk[0], s.codeq[...])
     to_corpus(s.cpart, s.crecv, s.c_s, s.c_r)
     s.crecv[c] = s.cpart[...]
     got(s.crecv.at[pl.ds(0, nc - 1)], s.c_r)
@@ -952,11 +957,10 @@
     sent(s.hall.at[:, pl.ds(0, 3)], s.h_s)
     sent(s.lsend.at[:, pl.ds(0, r - 1)], s.lr_s)
     sent(s.gsend.at[:, pl.ds(0, ng - 1)], s.g_s)
-    sent(s.t_recv.at[pl.ds(0, nq - 1)], s.t_s)
+    sent(s.t_recv.at[pl.ds(0, len(others))], s.t_s)
 
     @pl.when(g == q)
     def _():
-        sent(s.pp.at[pl.ds(0, r - 1)], s.pp_s)
         sent(s.pblk.at[pl.ds(0, nq - 1)], s.pb_s)
 
     @pl.when(g != q)
@@ -984,27 +988,27 @@
     nh = halves_of(ffc)
     hw = ffc // nh
     nu = nblk * nh
-    qm, lm, pm = bm // nq, bm // r, bm // nc
-    tb = nblk * pm
+    qm, gm = bm // nq, bm // ng
+    tb = nblk * gm
     nqueries = nq * lengths.shape[0]
     bits = code_weight.shape[1]
     bw = bits // nq
     vm, dma = pltpu.VMEM, pltpu.SemaphoreType.DMA
     scratch = dict(
-        gu=vm((2,) + gate_weight.shape, BF16), down=vm(down_weight.shape, BF16), codew=vm((2,) + code_weight.shape, BF16),
+        gu=vm((2,) + gate_weight.shape, BF16), down=vm(down_weight.shape, BF16), codeq=vm((w, bw), BF16), corp=vm(corpus_codes.shape, BF16),
         lens_s=pltpu.SMEM(lengths.shape, jnp.int32),
         hidq=vm((nq, slots, w // nq), BF16), colbuf=vm((nq, slots, w // nq), BF16), xpk=vm((nblk, bm, w // nq), BF16), lens_all=vm((nq, 8, slots), jnp.int32), xall=vm((r, nblk, nq, bm, w // nq), BF16),
         xn=vm((bm, dq), BF16), inv_c=vm((nblk, bm, LANES), F32),
         st_send=vm((8, slots), F32), st_recv=vm((nc, 8, slots), F32), inv_all=vm((nq, 8, slots), F32),
         psend=vm((nu, nq, 2, qm, hw), BF16), precv=vm((nu, 4, 2, qm, hw), BF16), pown=vm((nu, 2, qm, hw), F32), full=vm((nh, 2, bm, hw), F32),
         hall=vm((nu, nq, qm, hw), BF16),
-        lsend=vm((nblk, r, lm, dq), BF16), lrecv=vm((nblk, r, lm, dq), BF16),
-        gsend=vm((nblk, ng, pm, dq), BF16), grecv=vm((nblk, ng, pm, dq), BF16), res=vm((tb, dq), F32),
-        t_send=vm((tb, LANES), F32), t_recv=vm((nq, tb, LANES), F32),
-        pp=vm((r, nqueries, w), BF16), prc=vm((nc, nqueries, w), BF16), pblk=vm((nq, nqueries, w), BF16),
+        acc=vm((nblk, bm, dq), F32), lsend=vm((nblk, r, bm, w), BF16), lrecv=vm((nblk, r, bm, w), BF16),
+        mine=vm((nblk, bm, w), F32), gsend=vm((nblk, ng, gm, w), BF16), grecv=vm((nblk, ng, gm, w), BF16), res=vm((tb, w), F32),
+        t_send=vm((8, LANES), F32), t_recv=vm((nq * r, 8, LANES), F32),
+        pp=vm((nqueries, w), F32), prc=vm((ng, nqueries, w), F32), pblk=vm((nq, nqueries, w), BF16),
         cpart=vm((nqueries, bw), F32), crecv=vm((nc, nqueries, bw), F32), codes=vm((nq, nqueries, bw), BF16),
         top_q=vm((nq, nqueries, LANES), F32), top_c=vm((nc, nqueries, LANES), F32), board=vm((LANES, LANES), F32),
-        w_s=dma((5,)), l_s=dma, l_r=dma, a_s=dma, a_r=dma, st_s=dma, st_r=dma, iv_s=dma, iv_r=dma,
+        w_s=dma((6,)), l_s=dma, l_r=dma, a_s=dma, a_r=dma, st_s=dma, st_r=dma, iv_s=dma, iv_r=dma,
         x_s=dma, x_r=dma((nblk,)), la_s=dma, la_r=dma((nblk,)),
         p_s=dma, p_r=dma((nu,)), pf_r=dma((nu,)), h_s=dma, hn_r=dma((nu,)), hb_r=dma((nblk,)),
         lr_s=dma, lr_r=dma((nblk,)), g_s=dma, g_r=dma((nblk,)),
@@ -1029,7 +1033,7 @@
     nreal = nq * slots * REAL_NUM // REAL_DEN
     nqueries = nq * rest[0].shape[0]
     lists = nqueries * max(nc, nq, rest[5].shape[0] // LANES)
-    fits = lists <= LANES and LANES % lists == 0 and nreal % (8 * nc) == 0 and w % (nq * LANES) == 0 and rest[4].shape == rest[5].shape
+    fits = nreal // nq <= LANES and lists <= LANES and LANES % lists == 0 and nreal % (8 * nc) == 0 and w % (nq * LANES) == 0
     body = per_device_fast if fits else per_device_general
     return body(nq, nc, hidden_in, *rest)
 

time: 84.1 us -> 84.3 us (level)
  no operation moved by 1% of the time
where the time goes in v6:
time: 84.3 us; the launch traced here: 84.1 us
  Pallas kernels  82.8 us (98%)
  local copies, waits for them, and re-layouts  1.3 us (2%)
    pallas_call x1, Pallas kernels, per_device_fast(): pl.pallas_call(functools.partial(fast_kernel, dims, tuple(scratch)), out_...  82.8 us

profile of v6, /device:TPU:0, one launch (start us, length us, event | category | flops | bytes accessed | tf_op | source)
XLA Modules:
  0.0 84.1 jit_solution(3716181236495978791)
XLA Ops:
  0.0 82.8 %shard_map.73 = f32[16,100]{1,0:T(8,128)} custom-call(bf16[128,512]{1,0:T(8,128)(2,1)} %hid.1, s32[4]{0:T(128)} %lens.1, bf16[1024,1792]{1,0:T(8,128)(2,1)} %gate_h.1, bf16[1024,1792]{1,0:T(8,128)(2,1)} %up_h.1, bf16[1792,1024]{1,0:T(8,128)(2,1)} %down_h.1, bf16[512,1024]{1,0:T(8,128)(2,1)} %code_h.1, bf16[512,1024]{1,0:T(8,128)(2,1)} %corp_h.1), custom_call_target="tpu_custom_call" | custom-call | tf_op jit(solution)/shard_map/pallas_call | solution.py:1020
  82.8 1.3 %copy.9 = f32[16,100]{1,0:T(8,128)} copy(f32[16,100]{1,0:T(8,128)} %shard_map.73) | data formatting | bytes 12800

commit v7 on v6

--- a/solution.py
+++ b/solution.py
@@ -788,17 +788,22 @@
         s.precv[n, 3] = (s.psend[n, two].astype(F32) + s.precv[n, 2].astype(F32)).astype(BF16)
         passed_part(n).start()
 
+    split = (nh + 1) // 2
+
+    def landing(n):
+        return s.hb_r.at[2 * (n // nh) + lax.rem(n, nh) // split]
+
     def reduce_unit(n):
         got(s.precv.at[n, pl.ds(0, 2)], s.p_r.at[n])
         gsum = s.pown[n, 0] + s.precv[n, 0, 0].astype(F32) + s.precv[n, 1, 0].astype(F32)
         usum = s.pown[n, 1] + s.precv[n, 0, 1].astype(F32) + s.precv[n, 1, 1].astype(F32)
         s.hall[n, q] = (gsum / (1.0 + jnp.exp(-gsum)) * usum).astype(BF16)
         h_near(n, 0, s.hn_r.at[n]).start()
-        h_near(n, 1, s.hb_r.at[n // nh]).start()
+        h_near(n, 1, landing(n)).start()
 
     def relay_unit(n):
         got(s.hall.at[n, 0], s.hn_r.at[n])
-        h_pass(n, s.hb_r.at[n // nh]).start()
+        h_pass(n, landing(n)).start()
 
     def lane_send(b, k):
         t = lane(k)
@@ -810,9 +815,10 @@
 
     def down_block(b):
         part = None
-        got(s.hall.at[pl.ds(b * nh, nh), pl.ds(0, 2)], s.hb_r.at[b])
         for h in range(nh):
             n = b * nh + h
+            if h % split == 0:
+                got(s.hall.at[pl.ds(n, min(split, nh - h)), pl.ds(0, 2)], s.hb_r.at[2 * b + h // split])
             term = mm(s.hall[n].reshape(bm, hw), s.down[h * hw:(h + 1) * hw, :])
             part = term if part is None else part + term
         s.acc[b] = part
@@ -842,9 +848,8 @@
             fetch(b + 1)
 
     fetch(0)
-    stages = (products, fetch_next, functools.partial(units, pass_unit), functools.partial(units, reduce_unit),
-              functools.partial(units, relay_unit), down_block, sum_block)
-    delays = (0, 0, 1, 2, 3, 4, 5)
+    stages = (products, fetch_next, functools.partial(units, pass_unit), functools.partial(units, reduce_unit), functools.partial(units, relay_unit), sum_block, down_block)
+    delays = (0, 0, 1, 2, 3, 5, 4)
 
     def turn(t, carry):
         for stage, delay in zip(stages, delays):
@@ -854,7 +859,7 @@
         return carry
 
     loaded(s.down, 3)
-    lax.fori_loop(0, nblk + delays[-1], turn, 0)
+    lax.fori_loop(0, nblk + max(delays), turn, 0)
     own = pl.ds(pl.multiple_of(g * gm, gm), gm)
     for b in range(nblk):
         for k in range(nq):
@@ -973,8 +978,8 @@
     sent(s.top_c.at[pl.ds(0, nc - 1)], s.tc_s)
 
 
-def halves_of(ffc):
-    return 2 if ffc % (2 * LANES) == 0 else 1
+def chunks_of(ffc):
+    return ffc // CHUNK if ffc % CHUNK == 0 else 1
 
 
 def per_device_fast(nq, nc, hidden_in, lengths, gate_weight, up_weight, down_weight, code_weight, corpus_codes):
@@ -985,7 +990,7 @@
     dq, ffc = gate_weight.shape
     bm = 8 * nc
     nblk = nreal // bm
-    nh = halves_of(ffc)
+    nh = chunks_of(ffc)
     hw = ffc // nh
     nu = nblk * nh
     qm, gm = bm // nq, bm // ng
@@ -1010,7 +1015,7 @@
         top_q=vm((nq, nqueries, LANES), F32), top_c=vm((nc, nqueries, LANES), F32), board=vm((LANES, LANES), F32),
         w_s=dma((6,)), l_s=dma, l_r=dma, a_s=dma, a_r=dma, st_s=dma, st_r=dma, iv_s=dma, iv_r=dma,
         x_s=dma, x_r=dma((nblk,)), la_s=dma, la_r=dma((nblk,)),
-        p_s=dma, p_r=dma((nu,)), pf_r=dma((nu,)), h_s=dma, hn_r=dma((nu,)), hb_r=dma((nblk,)),
+        p_s=dma, p_r=dma((nu,)), pf_r=dma((nu,)), h_s=dma, hn_r=dma((nu,)), hb_r=dma((2 * nblk,)),
         lr_s=dma, lr_r=dma((nblk,)), g_s=dma, g_r=dma((nblk,)),
         t_s=dma, t_r=dma, pp_s=dma, pp_r=dma, pb_s=dma, pb_r=dma, c_s=dma, c_r=dma, o_s=dma, o_r=dma,
         tq_s=dma, tq_r=dma, tc_s=dma, tc_r=dma,

time: 84.3 us -> 83.4 us (0.989)
  Pallas kernels: 82.8 us -> 81.9 us
where the time goes in v7:
time: 83.4 us; the launch traced here: 83.2 us
  Pallas kernels  81.9 us (98%)
  local copies, waits for them, and re-layouts  1.3 us (2%)
    pallas_call x1, Pallas kernels, per_device_fast(): pl.pallas_call(functools.partial(fast_kernel, dims, tuple(scratch)), out_...  81.9 us

profile of v7, /device:TPU:0, one launch (start us, length us, event | category | flops | bytes accessed | tf_op | source)
XLA Modules:
  0.0 83.2 jit_solution(11911782704754295292)
XLA Ops:
  0.0 81.9 %shard_map.73 = f32[16,100]{1,0:T(8,128)} custom-call(bf16[128,512]{1,0:T(8,128)(2,1)} %hid.1, s32[4]{0:T(128)} %lens.1, bf16[1024,1792]{1,0:T(8,128)(2,1)} %gate_h.1, bf16[1024,1792]{1,0:T(8,128)(2,1)} %up_h.1, bf16[1792,1024]{1,0:T(8,128)(2,1)} %down_h.1, bf16[512,1024]{1,0:T(8,128)(2,1)} %code_h.1, bf16[512,1024]{1,0:T(8,128)(2,1)} %corp_h.1), custom_call_target="tpu_custom_call" | custom-call | tf_op jit(solution)/shard_map/pallas_call | solution.py:1025
  81.9 1.3 %copy.9 = f32[16,100]{1,0:T(8,128)} copy(f32[16,100]{1,0:T(8,128)} %shard_map.73) | data formatting | bytes 12800

commit v8 on v7

--- a/solution.py
+++ b/solution.py
@@ -731,17 +731,25 @@
         odd = lax.rem(n, 2)
         return side_a + (side_b - side_a) * odd, side_b + (side_a - side_b) * odd
 
+    split = (nh + 1) // 2
+
+    def group(n):
+        return 2 * (n // nh) + lax.rem(n, nh) // split
+
+    def several(n, h):
+        return pl.ds(n, min(split, nh - h))
+
     def near_part(n):
         one, _ = sides(n)
-        return rcopy(s.psend.at[n, one], s.precv.at[n, 0], s.p_s, s.p_r.at[n], (one, c))
+        return rcopy(s.psend.at[n, one], s.precv.at[n, 0], s.p_s, s.p_r.at[group(n)], (one, c))
 
     def far_part(n):
         one, _ = sides(n)
-        return rcopy(s.psend.at[n, far], s.precv.at[n, 2], s.p_s, s.pf_r.at[n], (one, c))
+        return rcopy(s.psend.at[n, far], s.precv.at[n, 2], s.p_s, s.pf_r.at[group(n)], (one, c))
 
     def passed_part(n):
         _, two = sides(n)
-        return rcopy(s.precv.at[n, 3], s.precv.at[n, 1], s.p_s, s.p_r.at[n], (two, c))
+        return rcopy(s.precv.at[n, 3], s.precv.at[n, 1], s.p_s, s.p_r.at[group(n)], (two, c))
 
     def h_near(n, k, sem):
         return rcopy(s.hall.at[n, q], s.hall.at[n, q], s.h_s, sem, (sides(n)[k], c))
@@ -782,28 +790,26 @@
             for e in range(2):
                 s.pown[n, e] = s.full[h, e, pl.ds(pl.multiple_of(q * qm, qm), qm)]
 
-    def pass_unit(n):
+    def pass_unit(n, h):
         _, two = sides(n)
-        got(s.precv.at[n, 2], s.pf_r.at[n])
+        if h % split == 0:
+            got(s.precv.at[several(n, h), 2], s.pf_r.at[group(n)])
         s.precv[n, 3] = (s.psend[n, two].astype(F32) + s.precv[n, 2].astype(F32)).astype(BF16)
         passed_part(n).start()
 
-    split = (nh + 1) // 2
-
-    def landing(n):
-        return s.hb_r.at[2 * (n // nh) + lax.rem(n, nh) // split]
-
-    def reduce_unit(n):
-        got(s.precv.at[n, pl.ds(0, 2)], s.p_r.at[n])
+    def reduce_unit(n, h):
+        if h % split == 0:
+            got(s.precv.at[several(n, h), pl.ds(0, 2)], s.p_r.at[group(n)])
         gsum = s.pown[n, 0] + s.precv[n, 0, 0].astype(F32) + s.precv[n, 1, 0].astype(F32)
         usum = s.pown[n, 1] + s.precv[n, 0, 1].astype(F32) + s.precv[n, 1, 1].astype(F32)
         s.hall[n, q] = (gsum / (1.0 + jnp.exp(-gsum)) * usum).astype(BF16)
-        h_near(n, 0, s.hn_r.at[n]).start()
-        h_near(n, 1, landing(n)).start()
-
-    def relay_unit(n):
-        got(s.hall.at[n, 0], s.hn_r.at[n])
-        h_pass(n, landing(n)).start()
+        h_near(n, 0, s.hn_r.at[group(n)]).start()
+        h_near(n, 1, s.hb_r.at[group(n)]).start()
+
+    def relay_unit(n, h):
+        if h % split == 0:
+            got(s.hall.at[several(n, h), 0], s.hn_r.at[group(n)])
+        h_pass(n, s.hb_r.at[group(n)]).start()
 
     def lane_send(b, k):
         t = lane(k)
@@ -818,7 +824,7 @@
         for h in range(nh):
             n = b * nh + h
             if h % split == 0:
-                got(s.hall.at[pl.ds(n, min(split, nh - h)), pl.ds(0, 2)], s.hb_r.at[2 * b + h // split])
+                got(s.hall.at[several(n, h), pl.ds(0, 2)], s.hb_r.at[group(n)])
             term = mm(s.hall[n].reshape(bm, hw), s.down[h * hw:(h + 1) * hw, :])
             part = term if part is None else part + term
         s.acc[b] = part
@@ -840,7 +846,7 @@
 
     def units(unit, b):
         for h in range(nh):
-            unit(b * nh + h)
+            unit(b * nh + h, h)
 
     def fetch_next(b):
         @pl.when(b + 1 < nblk)
@@ -1015,7 +1021,7 @@
         top_q=vm((nq, nqueries, LANES), F32), top_c=vm((nc, nqueries, LANES), F32), board=vm((LANES, LANES), F32),
         w_s=dma((6,)), l_s=dma, l_r=dma, a_s=dma, a_r=dma, st_s=dma, st_r=dma, iv_s=dma, iv_r=dma,
         x_s=dma, x_r=dma((nblk,)), la_s=dma, la_r=dma((nblk,)),
-        p_s=dma, p_r=dma((nu,)), pf_r=dma((nu,)), h_s=dma, hn_r=dma((nu,)), hb_r=dma((2 * nblk,)),
+        p_s=dma, p_r=dma((2 * nblk,)), pf_r=dma((2 * nblk,)), h_s=dma, hn_r=dma((2 * nblk,)), hb_r=dma((2 * nblk,)),
         lr_s=dma, lr_r=dma((nblk,)), g_s=dma, g_r=dma((nblk,)),
         t_s=dma, t_r=dma, pp_s=dma, pp_r=dma, pb_s=dma, pb_r=dma, c_s=dma, c_r=dma, o_s=dma, o_r=dma,
         tq_s=dma, tq_r=dma, tc_s=dma, tc_r=dma,

time: 83.4 us -> 82.9 us (level)
  no operation moved by 1% of the time
where the time goes in v8:
time: 82.9 us; the launch traced here: 82.7 us
  Pallas kernels  81.4 us (98%)
  local copies, waits for them, and re-layouts  1.3 us (2%)
    pallas_call x1, Pallas kernels, per_device_fast(): pl.pallas_call(functools.partial(fast_kernel, dims, tuple(scratch)), out_...  81.4 us

profile of v8, /device:TPU:0, one launch (start us, length us, event | category | flops | bytes accessed | tf_op | source)
XLA Modules:
  0.0 82.7 jit_solution(17757367219791016559)
XLA Ops:
  0.0 81.4 %shard_map.73 = f32[16,100]{1,0:T(8,128)} custom-call(bf16[128,512]{1,0:T(8,128)(2,1)} %hid.1, s32[4]{0:T(128)} %lens.1, bf16[1024,1792]{1,0:T(8,128)(2,1)} %gate_h.1, bf16[1024,1792]{1,0:T(8,128)(2,1)} %up_h.1, bf16[1792,1024]{1,0:T(8,128)(2,1)} %down_h.1, bf16[512,1024]{1,0:T(8,128)(2,1)} %code_h.1, bf16[512,1024]{1,0:T(8,128)(2,1)} %corp_h.1), custom_call_target="tpu_custom_call" | custom-call | tf_op jit(solution)/shard_map/pallas_call | solution.py:1031
  81.4 1.3 %copy.9 = f32[16,100]{1,0:T(8,128)} copy(f32[16,100]{1,0:T(8,128)} %shard_map.73) | data formatting | bytes 12800
